TPU v7x, 512 devices: a whole 4x8x8 slice. The times are simulated.
512 devices in a mesh: ent: 128 (over y, z, core), rep: 4 (over x).
Axes of the slice: x: 4, y: 8, z: 8, core: 2. Of those that a mesh axis runs over, the one named last changes fastest.
Arguments:
- entity_table: float32 [65536, 200], P('ent'), may hold values from -6 to 6
- relation_table: bfloat16 [822, 200], replicated, may hold values from -12 to 12
- filters: float32 [32, 9], replicated, may hold values from -2 to 2
- projection: bfloat16 [9728, 200], replicated, may hold values from -0.0625 to 0.0625
- request_owner: int32 [163840, 1], P(('ent', 'rep')), may hold values from 0 to 127; in each aligned block of 320 rows (0 to 319, 320 to 639, ...) at most 4 rows name the same one
- request_row: int32 [163840], P(('ent', 'rep')), may hold values from 0 to 511
- relation_id: int32 [65536], P(('ent', 'rep')), may hold values from 0 to 821
- rare_flag: int32 [65536], P('ent'), may hold values 0 or 1
- running_norm: float32 [], replicated, may hold values from 2 to 6
Outputs:
- new_table: float32 [65536, 200], P('ent')
- filter_grad: float32 [32, 9], replicated
Inputs may be any that keep to these rules, and one draw needn't show every extreme that they name: `request_owner`: among the requests of one device no owner shard is named more than 4 times, a bound that some block reaches.
All inputs are finite; a program needn't handle non-finite values. No bound on the sum of `rare_flag` on one device may be relied on, other than what follows from the above.
Results may differ from a plain program's by a relative error of at most 0.002.
Values sent between devices are 32-bit elements; how exact they have to be, the bound alone decides.
A program may use at most 64 MiB of HBM per device.

v0:
```python
import jax
import jax.numpy as jnp
from jax import lax
from jax.sharding import PartitionSpec as P

D = 200
ROWS = 20


learn_rate = 0.5
norm_eps = 1e-06


def conv_act(head_rows, rel_rows, filters):
    count = head_rows.shape[0]
    stacked = jnp.concatenate(
        [head_rows.reshape(count, ROWS, D // ROWS), rel_rows.reshape(count, ROWS, D // ROWS)],
        axis=1,
    )[:, None]
    kernel = filters.reshape(filters.shape[0], 1, 3, 3)
    conv_out = lax.conv_general_dilated(
        stacked, kernel, (1, 1), "VALID", precision=lax.Precision.HIGHEST
    )
    return jax.nn.silu(conv_out).reshape(count, -1)


def block_step(row_values, rel_rows, filters, projection, batch_rows, neg_count):
    head_rows = row_values[:batch_rows]
    pos_rows = row_values[batch_rows : 2 * batch_rows]
    neg_rows = row_values[2 * batch_rows :]
    activated, pullback = jax.vjp(
        lambda head_part, filt_part: conv_act(head_part, rel_rows, filt_part), head_rows, filters
    )
    features = activated.astype(jnp.bfloat16)
    projected = jnp.dot(features, projection, preferred_element_type=jnp.float32)
    sig_proj = jax.nn.sigmoid(projected)
    hidden = projected * sig_proj
    score_pos = jnp.sum(hidden * pos_rows, 1)
    score_neg = jnp.dot(hidden, neg_rows.T, precision=lax.Precision.HIGHEST)
    grad_pos = -jax.nn.sigmoid(-score_pos)
    grad_neg = jax.nn.sigmoid(score_neg) / neg_count
    pos_grad_rows = grad_pos[:, None] * hidden
    neg_grad_rows = jnp.dot(grad_neg.T, hidden, precision=lax.Precision.HIGHEST)
    grad_hidden = grad_pos[:, None] * pos_rows + jnp.dot(
        grad_neg, neg_rows, precision=lax.Precision.HIGHEST
    )
    grad_proj = (grad_hidden * sig_proj * (1.0 + projected * (1.0 - sig_proj))).astype(jnp.bfloat16)
    grad_feat = lax.dot_general(
        grad_proj, projection, (((1,), (1,)), ((), ())), preferred_element_type=jnp.float32
    )
    head_grad_rows, filter_part = pullback(grad_feat)
    return (jnp.concatenate([head_grad_rows, pos_grad_rows, neg_grad_rows], axis=0), filter_part)


def body(
    entity_table,
    relation_table,
    filters,
    projection,
    request_owner,
    request_row,
    relation_id,
    rare_flag,
    running_norm,
):
    ent_count = lax.axis_size("ent")
    rep_count = lax.axis_size("rep")
    req_count = request_row.shape[0]
    batch_rows = relation_id.shape[0]
    neg_count = req_count - 2 * batch_rows
    width = entity_table.shape[1]
    slots_each = max(2, 3 * req_count // (2 * ent_count) + 1)
    owner_shard = request_owner[:, 0]
    onehot = (owner_shard[:, None] == jnp.arange(ent_count, dtype=jnp.int32)[None, :]).astype(
        jnp.int32
    )
    slot_index = jnp.sum(jnp.cumsum(onehot, 0) * onehot, 1) - 1
    slot_place = owner_shard * slots_each + slot_index
    send_ids = (
        jnp.zeros((ent_count * slots_each,), jnp.int32)
        .at[slot_place]
        .set(request_row)
        .reshape(ent_count, slots_each)
    )
    wanted = lax.all_to_all(send_ids, "ent", split_axis=0, concat_axis=0, tiled=True)
    found_rows = entity_table[wanted]
    fetched = lax.all_to_all(found_rows, "ent", split_axis=0, concat_axis=0, tiled=True)
    row_values = fetched.reshape(-1, width)[slot_place]
    rel_rows = relation_table[relation_id].astype(jnp.float32)
    grads, filter_part = block_step(
        row_values, rel_rows, filters, projection, batch_rows, neg_count
    )
    send_grads = (
        jnp.zeros((ent_count * slots_each, width), jnp.float32)
        .at[slot_place]
        .set(grads)
        .reshape(ent_count, slots_each, width)
    )
    received = lax.all_to_all(send_grads, "ent", split_axis=0, concat_axis=0, tiled=True)
    all_ids = lax.all_gather(wanted, "rep", axis=0, tiled=True)
    all_grads = lax.all_gather(received, "rep", axis=0, tiled=True)
    summed_grad = (
        jnp.zeros(entity_table.shape, jnp.float32)
        .at[all_ids.reshape(-1)]
        .add(all_grads.reshape(-1, width))
    )
    updated = entity_table - learn_rate * summed_grad
    row_norms = jnp.sqrt(jnp.sum(updated * updated, 1) + norm_eps)
    local_norm = jnp.sum(row_norms)
    filter_total = lax.psum(filter_part, ("ent", "rep"))
    norm_total = lax.psum(local_norm, "ent")
    filter_grad = filter_total / (batch_rows * ent_count * rep_count)
    target = 0.25 * running_norm + 0.75 * norm_total / (entity_table.shape[0] * ent_count)
    new_table = jnp.where(
        (rare_flag == 1)[:, None], updated * (target / row_norms)[:, None], updated
    )
    return (new_table, filter_grad)


def solution(mesh):
    in_specs = (
        P("ent", None),
        P(),
        P(),
        P(),
        P(("ent", "rep"), None),
        P(("ent", "rep")),
        P(("ent", "rep")),
        P("ent"),
        P(),
    )
    out_specs = (P("ent", None), P())
    return jax.shard_map(body, mesh=mesh, in_specs=in_specs, out_specs=out_specs, check_vma=False)
```

profile of v0, /device:TPU:1, one launch (start us, length us, event | category | flops | bytes accessed | tf_op | source)
XLA Modules:
  0.0 538.2 jit_solution(8350565503353187962)
XLA Ops:
  7.2 0.7 reduce
  7.9 0.1 iota_compare_fusion
  8.0 0.0 copy-start.5
  8.0 0.1 fusion.9
  8.3 0.2 fusion.15
  8.5 0.0 copy-start.6
  8.5 0.7 fusion.22
  9.2 0.0 copy-start.7
  9.2 3.1 scatter_custom_fusion
  12.3 0.7 all_to_all.16
  13.1 18.4 %all-to-all-start = ((s32[128,1,4]{2,1,0:T(1,128)}), s32[128,1,4]{2,1,0:T(1,128)S(1)}, u32[]{:S(2)}, u32[]{:S(2)}) async-start(s32[128,1,4]{2,1,0:T(1,128)} %bitcast.4), calls=%async_computation | async-start | bytes 131072 | tf_op jit(solution)/shard_map/all_to_all | solution.py:85
  31.5 1.2 copy.117
  32.7 10.2 %all-to-all-done = s32[128,1,4]{2,1,0:T(1,128)S(1)} async-done(((s32[128,1,4]{2,1,0:T(1,128)}), s32[128,1,4]{2,1,0:T(1,128)S(1)}, u32[]{:S(2)}, u32[]{:S(2)}) %all-to-all-start) | async-done | bytes 2080 | tf_op jit(solution)/shard_map/all_to_all | solution.py:85
  43.0 0.1 reshape.145
  43.1 0.5 copy-done.2
  43.6 1.6 gather_fusion
  45.1 0.9 reshape.144
  46.1 5.7 %all-to-all-start.1 = ((f32[128,4,200]{2,1,0:T(4,128)}), f32[128,4,200]{2,1,0:T(4,128)S(1)}, u32[]{:S(2)}, u32[]{:S(2)}) async-start(f32[128,4,200]{2,1,0:T(4,128)} %reshape.144), calls=%async_computation.1 | async-start | bytes 1048576 | tf_op jit(solution)/shard_map/all_to_all | solution.py:87
  51.8 0.5 all-gather.3.cloned.1.call-start
  52.3 0.2 copy.100
  52.6 0.8 gather_fusion.2
  53.4 0.1 copy.101
  53.6 17.8 %all-to-all-done.1 = f32[128,4,200]{2,1,0:T(4,128)S(1)} async-done(((f32[128,4,200]{2,1,0:T(4,128)}), f32[128,4,200]{2,1,0:T(4,128)S(1)}, u32[]{:S(2)}, u32[]{:S(2)}) %all-to-all-start.1) | async-done | bytes 409632 | tf_op jit(solution)/shard_map/all_to_all | solution.py:87
  71.4 0.2 reshape.133
  71.6 1.6 gather_fusion.1
  73.2 0.7 fusion.28
  73.9 0.1 copy.99
  74.0 0.1 copy.136
  74.1 7.1 %multiply_convert_fusion = (bf16[128,32,38,8]{0,1,3,2:T(8,128)(2,1)S(1)}, f32[128,32,38,8]{0,1,3,2:T(8,128)}) fusion(f32[32,1,3,3]{0,1,3,2:T(1,128)S(1)} %reshape.195, f32[128,1,40,10]{0,2,3,1:T(8,128)S(1)} %bitcast.46), kind=kOutput, calls=%fused_computation.9 | convolution fusion | flops 140705792 | bytes 7677056 | tf_op jit(solution)/shard_map/jvp()/conv_general_dilated | solution.py:21
  81.2 1.0 copy.105
  82.1 1.6 copy.123
  83.8 3.5 multiply_reduce_fusion.1
  87.2 0.3 fusion.8
  87.5 0.0 slice-start
  87.6 0.3 fusion.25
  87.9 0.4 fusion.4
  88.3 0.0 slice-start.1
  88.3 2.0 fusion.30
  90.4 0.0 slice-done
  90.4 0.0 slice-done.1
  90.4 2.6 fusion.1
  93.1 2.2 copy-done
  95.3 23.1 %fusion.29 = f32[128,1,40,10]{0,1,3,2:T(1,128)S(1)} fusion(f32[128,32,38,8]{0,1,3,2:T(8,128)S(1)} %fusion.1, f32[32,1,3,3]{0,1,3,2:T(1,128)S(1)} %reshape.195), kind=kOutput, calls=%fused_computation.68 | convolution fusion | flops 134479872 | bytes 5186688 | tf_op jit(solution)/shard_map/transpose(jvp())/conv_general_dilated | solution.py:21
  118.5 0.1 copy.114
  118.7 1.9 scatter_custom_fusion.1
  120.6 0.2 reshape.138
  120.7 26.3 %all_to_all.25 = f32[128,4,200]{2,1,0:T(4,128)S(1)} all-to-all(f32[128,4,200]{2,1,0:T(4,128)S(1)} %reshape.138), channel_id=1, replica_groups=mesh['ent'=128,'rep'=4] {'ent'}, dimensions={0} | all-to-all | bytes 819200 | tf_op jit(solution)/shard_map/all_to_all | solution.py:99
  147.0 1.0 copy.115
  148.0 0.0 all-gather.3.cloned.1.call-update
  148.7 0.1 copy.96
  148.7 8.4 %all-gather = s32[512,1,4]{0,2,1:T(4,128)S(1)} all-gather(s32[128,1,4]{0,2,1:T(4,128)S(1)} %copy.96), channel_id=2, replica_groups=mesh['ent'=128,'rep'=4] {'rep'}, dimensions={0}, use_global_device_ids=true | all-gather | bytes 10240 | tf_op jit(solution)/shard_map/all_gather | solution.py:100
  157.2 0.1 copy.97
  157.3 0.2 reshape.132
  157.5 9.4 %convolution_reduce_fusion = f32[32,3,3]{0,2,1:T(4,128)S(1)} fusion(f32[128,32,38,8]{0,1,3,2:T(8,128)} %copy-done, f32[128,1,40,10]{0,2,3,1:T(8,128)S(1)} %bitcast.47), kind=kOutput, calls=%fused_computation.20 | convolution fusion | flops 134479872 | bytes 5186688 | tf_op jit(solution)/shard_map/transpose(jvp())/conv_general_dilated | solution.py:21
  166.9 97.7 %psum.15 = f32[32,9]{0,1:T(8,128)S(1)} all-reduce(f32[32,9]{0,1:T(8,128)S(1)} %reshape.140), channel_id=1, replica_groups=mesh['ent'=128,'rep'=4] {'ent','rep'}, use_global_device_ids=true, to_apply=%region_10.11 | all-reduce | flops 288 | bytes 2304 | tf_op jit(solution)/shard_map/psum | solution.py:110
  264.6 2.0 copy.116
  266.6 1.8 reshape.187
  268.3 12.1 %scatter_custom_fusion.2 = f32[512,200]{1,0:T(8,128)S(1)} fusion(s32[2048]{0:T(1024)S(1)} %bitcast.53, f32[2048,200]{1,0:T(8,128)} %reshape.187, f32[]{:T(128)} %constant.16.clone.1), kind=kCustom, calls=%fused_computation.28 | custom fusion | flops 409600 | bytes 410112 | tf_op jit(solution)/shard_map/scatter-add | solution.py:105
  280.4 0.2 multiply_reduce_fusion
  280.6 0.6 sqrt_reduce_fusion
  281.2 0.6 broadcast_multiply_fusion.1
  281.8 247.5 %psum.14 = f32[]{:T(128)} all-reduce(f32[]{:T(128)} %sqrt_reduce_fusion), channel_id=1, replica_groups=mesh['ent'=128,'rep'=4] {'ent'}, use_global_device_ids=true, to_apply=%region_9.10 | all-reduce | flops 1 | bytes 8 | tf_op jit(solution)/shard_map/psum | solution.py:111
  529.9 0.2 multiply_select_fusion
  530.1 0.9 copy.119
  (43 shorter events, 0.4 us)
Async XLA Ops:
  8.0 44.3 %copy-start.5 = (bf16[822,200]{0,1:T(8,128)(2,1)S(1)}, bf16[822,200]{0,1:T(8,128)(2,1)}, u32[]{:S(2)}) copy-start(bf16[822,200]{0,1:T(8,128)(2,1)} %param.10) | copy-start | bytes 986404
  8.2 44.3 %copy-start.9 = (s32[128]{0:T(128)S(1)}, s32[128]{0:T(128)}, u32[]{:S(2)}) copy-start(s32[128]{0:T(128)} %param.15) | copy-start | bytes 1540
  8.5 45.1 %copy-start.6 = (f32[32,9]{0,1:T(8,128)S(1)}, f32[32,9]{0,1:T(8,128)}, u32[]{:S(2)}) copy-start(f32[32,9]{0,1:T(8,128)} %param.11) | copy-start | bytes 3460
  9.2 62.3 %copy-start.7 = (s32[320]{0:T(512)}, s32[320]{0:T(512)S(1)}, u32[]{:S(2)}) copy-start(s32[320]{0:T(512)S(1)} %fusion.22) | copy-start | bytes 3844
  13.1 29.9 %all-to-all-start = ((s32[128,1,4]{2,1,0:T(1,128)}), s32[128,1,4]{2,1,0:T(1,128)S(1)}, u32[]{:S(2)}, u32[]{:S(2)}) async-start(s32[128,1,4]{2,1,0:T(1,128)} %bitcast.4), calls=%async_computation | async-start | bytes 131072 | tf_op jit(solution)/shard_map/all_to_all | solution.py:85
  42.9 0.6 copy-start.2
  46.1 25.3 %all-to-all-start.1 = ((f32[128,4,200]{2,1,0:T(4,128)}), f32[128,4,200]{2,1,0:T(4,128)S(1)}, u32[]{:S(2)}, u32[]{:S(2)}) async-start(f32[128,4,200]{2,1,0:T(4,128)} %reshape.144), calls=%async_computation.1 | async-start | bytes 1048576 | tf_op jit(solution)/shard_map/all_to_all | solution.py:87
  51.8 212.8 %all-gather.3.cloned.1.call-start = ((), (), s32[]{:S(2)}) async-start(), calls=%async_computation.3 | async-start | bytes 2048000 | tf_op jit(solution)/shard_map/all_gather | solution.py:101
  83.8 4.1 copy-start.4
  83.8 4.5 copy-start.1
  87.5 2.8 slice-start
  88.3 2.1 slice-start.1
  93.1 2.2 copy-start
  95.3 53.4 %copy-start.8 = (s32[512]{0:T(512)S(1)}, s32[512]{0:T(512)}, u32[]{:S(2)}) copy-start(s32[512]{0:T(512)} %param.16) | copy-start | bytes 6148
  95.3 53.4 %copy-start.3 = (s32[128,1,4]{2,1,0:T(1,128)S(1)}, s32[128,1,4]{2,1,0:T(1,128)}, u32[]{:S(2)}) copy-start(s32[128,1,4]{2,1,0:T(1,128)} %copy-done.2) | copy-start | bytes 6148
Sparse Core Ops, SparseCore 0:
  148.1 28.8 all-gather.2
where the time goes:
time: 544 us; the launch traced here: 538 us
  blocking collectives  380 us (70%)
  matrix products  46 us (8%)
  waiting for transfers between devices  28 us (5%)
  local copies, waits for them, and re-layouts  25.1 us (5%)
  starting transfers between devices  24.6 us (5%)
  other arithmetic  18.4 us (3%)
  between operations  16.1 us (3%)
    psum x1, blocking collectives, body(): norm_total = lax.psum(local_norm, 'ent')  247 us
    psum x1, blocking collectives, body(): filter_total = lax.psum(filter_part, ('ent', 'rep'))  97.7 us
    conv_general_dilated x3, matrix products, conv_act(): lax.conv_general_dilated(stacked, kernel, (1, 1), 'VALID', precision=lax....  39.5 us
    all_to_all x1, blocking collectives, body(): lax.all_to_all(send_grads, 'ent', split_axis=0, concat_axis=0, tiled=True)  26.3 us
    all_to_all x1, starting transfers between devices, body(): lax.all_to_all(send_ids, 'ent', split_axis=0, concat_axis=0, tiled=True)  18.4 us
    all_to_all x1, waiting for transfers between devices, body(): lax.all_to_all(found_rows, 'ent', split_axis=0, concat_axis=0, tiled=True)  17.8 us
    scatter-add x1, other arithmetic, body(): summed_grad = jnp.zeros(entity_table.shape, jnp.float32).at[all_ids.resha...  12.1 us
  transfers between devices with their start and end apart: 3, of which 2 were waited for; matrix products, arithmetic and copies ran while one was open for 2% of the time, Pallas kernels for 0%

commit v1 on v0

v1 whole, which is shorter than its diff:
```python
import functools
import jax
import jax.numpy as jnp
from jax import lax
from jax.experimental import pallas as pl
from jax.experimental.pallas import tpu as pltpu
from jax.sharding import PartitionSpec as P

MESH = pl.DeviceIdType.MESH
HI = lax.Precision.HIGHEST
F32, BF16, I32 = jnp.float32, jnp.bfloat16, jnp.int32
NT = (((1,), (1,)), ((), ()))
TN = (((0,), (0,)), ((), ()))


def iota(shape, dim):
    return lax.broadcasted_iota(I32, shape, dim)


def split(v):
    high = v.astype(BF16)
    return high, (v - high.astype(F32)).astype(BF16)


def mm(a, b, dims=(((1,), (0,)), ((), ()))):
    return lax.dot_general(a, b, dims, preferred_element_type=F32)


def slot_column(ids, ent, cap):
    slots = ent * cap
    rep = (iota((slots, ent), 0) // cap == iota((slots, ent), 1)).astype(F32)
    spread = lax.dot_general(rep, ids, (((1,), (0,)), ((), ())), precision=HI, preferred_element_type=F32)
    keep = iota((slots, 128), 0) % cap == iota((slots, 128), 1)
    return jnp.sum(jnp.where(keep, spread, 0.0), 1, keepdims=True)


def fetch_kernel(ent, cap, owner_ref, row_ref, table_ref, fetched_ref, ids_ref, slot_ref,
                 send_ids, got_ids, found, id_send, id_recv, row_send, row_recv):
    me, rep = lax.axis_index("ent"), lax.axis_index("rep")
    req = owner_ref.shape[1]
    width, rows = table_ref.shape
    barrier = pltpu.get_barrier_semaphore()

    def greet(i, c):
        pl.semaphore_signal(barrier, inc=1, device_id=((me + i) % ent, rep), device_id_type=MESH)
        return c

    lax.fori_loop(1, ent, greet, 0)
    owner = owner_ref[...]
    named = iota((ent, req), 0) == owner
    named_b = named.astype(F32).astype(BF16)
    before = (iota((req, req), 0) < iota((req, req), 1)).astype(F32).astype(BF16)
    rank = jnp.sum(jnp.where(named, mm(named_b, before), 0.0), 0, keepdims=True)
    slot_ref[...] = owner * cap + rank.astype(I32)
    marked = jnp.where(iota((128, req), 0).astype(F32) == rank, row_ref[...].astype(F32), 0.0)
    ids = lax.dot_general(named.astype(F32), marked, NT, precision=HI, preferred_element_type=F32)
    send_ids[...] = ids.reshape(ent, 1, 128)
    got_ids[pl.ds(me, 1)] = send_ids[pl.ds(me, 1)]
    pl.semaphore_wait(barrier, ent - 1)

    def send_id(i, c):
        p = (me + i) % ent
        pltpu.make_async_remote_copy(
            src_ref=send_ids.at[p], dst_ref=got_ids.at[me], send_sem=id_send, recv_sem=id_recv,
            device_id=(p, rep), device_id_type=MESH).start()
        return c

    lax.fori_loop(1, ent, send_id, 0)
    high, low = split(table_ref[...])
    others = pl.ds(0, ent - 1)
    pltpu.make_async_copy(got_ids.at[others], got_ids.at[others], id_recv).wait()
    got = got_ids[...].reshape(ent, 128)
    ids_ref[...] = got
    hot = (iota((ent * cap, rows), 1).astype(F32) == slot_column(got, ent, cap)).astype(F32).astype(BF16)
    picked = mm(hot, high, NT) + mm(hot, low, NT)
    found[...] = picked.reshape(ent, cap, width)

    def send_row(i, c):
        p = (me + i) % ent
        pltpu.make_async_remote_copy(
            src_ref=found.at[p], dst_ref=fetched_ref.at[me], send_sem=row_send, recv_sem=row_recv,
            device_id=(p, rep), device_id_type=MESH).start()
        return c

    lax.fori_loop(1, ent, send_row, 0)
    fetched_ref[pl.ds(me, 1)] = found[pl.ds(me, 1)]
    pltpu.make_async_copy(send_ids.at[others], send_ids.at[others], id_send).wait()
    pltpu.make_async_copy(found.at[others], found.at[others], row_send).wait()
    pltpu.make_async_copy(fetched_ref.at[others], fetched_ref.at[others], row_recv).wait()


def fetch(owner, row, table_t, ent, cap):
    width, rows = table_t.shape
    req = owner.shape[1]
    vmem = pl.BlockSpec(memory_space=pltpu.VMEM)
    return pl.pallas_call(
        functools.partial(fetch_kernel, ent, cap),
        out_shape=(jax.ShapeDtypeStruct((ent, cap, width), F32), jax.ShapeDtypeStruct((ent, 128), F32),
                   jax.ShapeDtypeStruct((1, req), I32)),
        in_specs=[vmem] * 3, out_specs=(vmem,) * 3,
        scratch_shapes=[pltpu.VMEM((ent, 1, 128), F32), pltpu.VMEM((ent, 1, 128), F32),
                        pltpu.VMEM((ent, cap, width), F32)] + [pltpu.SemaphoreType.DMA] * 4,
        compiler_params=pltpu.CompilerParams(collective_id=0, has_side_effects=True, vmem_limit_bytes=24 << 20),
        name="fetch",
    )(owner, row, table_t)
FILT, OUT_ROWS, OUT_COLS, IMG_ROWS, IMG_COLS, PITCH = 32, 38, 8, 40, 10, 16
HEAD_ROWS = 20


def tap_masks():
    r, k = iota((16, 64), 0), iota((16, 64), 1)
    di, dj = k // PITCH - r // OUT_COLS, k % PITCH - r % OUT_COLS
    return [((di == t // 3) & (dj == t % 3)).astype(F32) for t in range(9)]


def band_matrix(filt):
    total = jnp.zeros((FILT, 16, 64), F32)
    for t, mask in enumerate(tap_masks()):
        total = total + filt[:, t : t + 1][:, :, None] * mask[None]
    return total.reshape(FILT * 16, 64)


def fill_image(img_ref, base, value_ref, rows):
    for r in range(rows):
        img_ref[pl.ds(PITCH * (base + r), IMG_COLS), :] = value_ref[pl.ds(IMG_COLS * r, IMG_COLS), :]


def compute_kernel(fetched_ref, slot_ref, rel_ref, relid_ref, filt_ref, projt_ref, proj_ref,
                   send_ref, fgrad_ref, val, img, hi_img, lo_img, feat, dact, dimg, grads, strip):
    req, batch = slot_ref.shape[1], relid_ref.shape[1]
    slots = fetched_ref.shape[0]
    width = fetched_ref.shape[1]
    neg = req - 2 * batch
    hot = (iota((slots, req), 0) == slot_ref[...]).astype(F32).astype(BF16)
    high, low = split(fetched_ref[...])
    val[...] = mm(high, hot, TN) + mm(low, hot, TN)
    rels = rel_ref.shape[1]
    pick = (iota((rels, batch), 0) == relid_ref[...]).astype(F32).astype(BF16)
    img[...] = jnp.zeros(img.shape, F32)
    strip[...] = mm(rel_ref[...], pick)
    fill_image(img, HEAD_ROWS, strip, HEAD_ROWS)
    strip[...] = val[:, pl.ds(0, batch)]
    fill_image(img, 0, strip, HEAD_ROWS)
    h, l = split(img[...])
    hi_img[...] = h
    lo_img[...] = l
    band = band_matrix(filt_ref[...])
    bh, bl = split(band)
    lhs = jnp.concatenate([bh, bh, bl], 1)

    def conv(q, c):
        at = pl.ds(pl.multiple_of(q * 2 * PITCH, 2 * PITCH), 4 * PITCH)
        hi, lo = hi_img[at, :], lo_img[at, :]
        v = mm(lhs, jnp.concatenate([hi, lo, hi], 0))
        s = 0.5 * jnp.tanh(0.5 * v) + 0.5
        a = v * s
        out = pl.ds(pl.multiple_of(q * 16, 16), 16)
        feat[:, out, :] = a.astype(BF16).reshape(FILT, 16, batch)
        dact[:, out, :] = (s + a * (1.0 - s)).reshape(FILT, 16, batch)
        return c

    lax.fori_loop(0, OUT_ROWS // 2, conv, 0)
    projected = mm(projt_ref[...], feat[...].reshape(FILT * OUT_ROWS * OUT_COLS, batch))
    sig = 0.5 * jnp.tanh(0.5 * projected) + 0.5
    hidden = projected * sig
    pos, negs = val[:, pl.ds(batch, batch)], val[:, pl.ds(2 * batch, neg)]
    dot_hi = functools.partial(lax.dot_general, precision=HI, preferred_element_type=F32)
    score_pos = jnp.sum(hidden * pos, 0, keepdims=True)
    score_neg = dot_hi(negs, hidden, TN)
    grad_pos = -jax.nn.sigmoid(-score_pos)
    grad_neg = jax.nn.sigmoid(score_neg) / neg
    grads[:, pl.ds(batch, batch)] = grad_pos * hidden
    grads[:, pl.ds(2 * batch, neg)] = dot_hi(hidden, grad_neg, NT)
    grad_hidden = grad_pos * pos + dot_hi(negs, grad_neg, (((1,), (0,)), ((), ())))
    grad_proj = (grad_hidden * sig * (1.0 + projected * (1.0 - sig))).astype(BF16)
    dimg[...] = jnp.zeros(dimg.shape, F32)
    acc0 = jnp.zeros((FILT * 16, 128), F32)

    def back(q, acc):
        out = pl.ds(pl.multiple_of(q * 16, 16), 16)
        at = pl.ds(pl.multiple_of(q * 2 * PITCH, 2 * PITCH), 4 * PITCH)
        pr = proj_ref[:, out, :].reshape(FILT * 16, width)
        d = mm(pr, grad_proj) * dact[:, out, :].reshape(FILT * 16, batch)
        dh, dl = split(d)
        hi, lo = hi_img[at, :], lo_img[at, :]
        left = jnp.concatenate([dh, dl], 1)
        zero = jnp.zeros_like(lo)
        right = jnp.concatenate([jnp.concatenate([hi, hi], 1), jnp.concatenate([lo, zero], 1)], 0)
        acc = acc + mm(left, right, NT)

        @pl.when(q < HEAD_ROWS // 2)
        def _():
            part = mm(jnp.concatenate([bh, bl], 1), dh, TN)
            dimg[at, :] += part[:64] + part[64:] + mm(bh, dl, TN)

        return acc

    acc = lax.fori_loop(0, OUT_ROWS // 2, back, acc0)
    for r in range(HEAD_ROWS):
        strip[pl.ds(IMG_COLS * r, IMG_COLS), :] = dimg[pl.ds(PITCH * r, IMG_COLS), :]
    grads[:, pl.ds(0, batch)] = strip[...]
    joint = (acc[:, :64] + acc[:, 64:]).reshape(FILT, 16, 64)
    fgrad_ref[...] = jnp.zeros(fgrad_ref.shape, F32)
    for t, mask in enumerate(tap_masks()):
        fgrad_ref[t : t + 1, :FILT] = jnp.sum(jnp.sum(joint * mask[None], 1), 1).reshape(1, FILT)
    gh, gl = split(grads[...])
    send_ref[...] = mm(hot, gh, NT) + mm(hot, gl, NT)


def compute(fetched, slot, rel_t, relid, filt, proj_t, proj):
    slots, width = fetched.shape
    req, batch, feats = slot.shape[1], relid.shape[1], proj.shape[0]
    per = OUT_ROWS * OUT_COLS
    vmem = pl.BlockSpec(memory_space=pltpu.VMEM)
    return pl.pallas_call(
        compute_kernel,
        out_shape=(jax.ShapeDtypeStruct((slots, width), F32), jax.ShapeDtypeStruct((16, 128), F32)),
        in_specs=[vmem] * 7, out_specs=(vmem,) * 2,
        scratch_shapes=[pltpu.VMEM((width, req), F32), pltpu.VMEM((IMG_ROWS * PITCH, batch), F32),
                        pltpu.VMEM((IMG_ROWS * PITCH, batch), BF16), pltpu.VMEM((IMG_ROWS * PITCH, batch), BF16),
                        pltpu.VMEM((FILT, per, batch), BF16), pltpu.VMEM((FILT, per, batch), F32),
                        pltpu.VMEM((HEAD_ROWS * PITCH + 2 * PITCH, batch), F32), pltpu.VMEM((width, req), F32),
                        pltpu.VMEM((width, batch), F32)],
        compiler_params=pltpu.CompilerParams(vmem_limit_bytes=40 << 20),
        name="triples",
    )(fetched, slot, rel_t, relid, filt, proj_t, proj.reshape(FILT, per, width))
learn_rate, norm_eps = 0.5, 1e-06
NORM_ROW = 9


def merge_kernel(ent, reps, cap, group, grads_ref, ids_ref, table_ref, small_ref, rare_ref, run_ref,
                 out_ref, total_ref, land, part, pland, upd, s_here, s_x, s_g, s_y, row_send, row_recv,
                 part_send, part_recv, upd_send, upd_recv, sx_send, sx_recv, sg_send, sg_recv, sy_send, sy_recv):
    me, rep = lax.axis_index("ent"), lax.axis_index("rep")
    width, rows = table_ref.shape
    piece = rows // reps
    outer = ent // group
    y, g = me // group, me % group
    barrier = pltpu.get_barrier_semaphore()

    def loop(start, stop, step):
        lax.fori_loop(start, stop, lambda i, c: (step(i), c)[1], 0)

    def remote(src, dst, send, recv, p, r):
        pltpu.make_async_remote_copy(src_ref=src, dst_ref=dst, send_sem=send, recv_sem=recv,
                                     device_id=(p, r), device_id_type=MESH).start()

    def drain(ref, count, sem):
        at = ref.at[pl.ds(0, count)]
        pltpu.make_async_copy(at, at, sem).wait()

    def columns(r):
        return pl.ds(pl.multiple_of(r * piece, piece), piece)

    loop(1, ent, lambda i: pl.semaphore_signal(barrier, inc=1, device_id=((me + i) % ent, rep), device_id_type=MESH))
    loop(1, reps, lambda i: pl.semaphore_signal(barrier, inc=1, device_id=(me, (rep + i) % reps), device_id_type=MESH))
    pl.semaphore_wait(barrier, ent + reps - 2)

    def send_row(i):
        p = (me + i) % ent
        remote(grads_ref.at[p], land.at[me], row_send, row_recv, p, rep)

    loop(1, ent, send_row)
    land[pl.ds(me, 1)] = grads_ref[pl.ds(me, 1)]
    hot = (iota((ent * cap, rows), 1).astype(F32) == slot_column(ids_ref[...], ent, cap)).astype(F32).astype(BF16)
    drain(grads_ref, ent - 1, row_send)
    drain(land, ent - 1, row_recv)
    high, low = split(land[...].reshape(ent * cap, width))
    sums = mm(high, hot, TN) + mm(low, hot, TN)
    for r in range(reps):
        part[r] = sums[:, r * piece : (r + 1) * piece]
    pland[pl.ds(rep, 1)] = part[pl.ds(rep, 1)]
    loop(1, reps, lambda i: remote(part.at[(rep + i) % reps], pland.at[rep], part_send, part_recv, me, (rep + i) % reps))
    drain(part, reps - 1, part_send)
    drain(pland, reps - 1, part_recv)
    block = table_ref[:, columns(rep)] - learn_rate * jnp.sum(pland[...], 0)
    upd[:, columns(rep)] = block
    mine = upd.at[:, columns(rep)]
    norms = jnp.sqrt(jnp.sum(block * block, 0, keepdims=True) + norm_eps)
    here = jnp.where(iota((16, piece), 0) == NORM_ROW, norms, small_ref[...])
    s_here[0] = here
    s_x[pl.ds(rep, 1)] = here[None]
    loop(1, reps, lambda i: remote(s_here.at[0], s_x.at[rep], sx_send, sx_recv, me, (rep + i) % reps))
    loop(1, reps, lambda i: remote(mine, upd.at[:, columns(rep)], upd_send, upd_recv, me, (rep + i) % reps))
    drain(s_x, reps - 1, sx_recv)
    s_here[1] = jnp.sum(s_x[...], 0)
    s_g[pl.ds(g, 1)] = s_here[pl.ds(1, 1)]
    loop(1, group, lambda i: remote(s_here.at[1], s_g.at[g], sg_send, sg_recv, y * group + (g + i) % group, rep))
    drain(s_g, group - 1, sg_recv)
    s_here[2] = jnp.sum(s_g[...], 0)
    s_y[pl.ds(y, 1)] = s_here[pl.ds(2, 1)]
    loop(1, outer, lambda i: remote(s_here.at[2], s_y.at[y], sy_send, sy_recv, (y + i) % outer * group + g, rep))
    drain(s_y, outer - 1, sy_recv)
    total = jnp.sum(s_y[...], 0)
    total_ref[...] = total
    norm_total = jnp.sum(total[NORM_ROW : NORM_ROW + 1, :], 1, keepdims=True)
    target = 0.25 * run_ref[...] + 0.75 * norm_total / (rows * ent)
    drain(s_x, reps - 1, sx_send)
    drain(s_g, group - 1, sg_send)
    drain(s_y, outer - 1, sy_send)
    three = upd.at[:, pl.ds(0, (reps - 1) * piece)]
    pltpu.make_async_copy(three, three, upd_send).wait()
    pltpu.make_async_copy(three, three, upd_recv).wait()
    updated = upd[...]
    norm = jnp.sqrt(jnp.sum(updated * updated, 0, keepdims=True) + norm_eps)
    out_ref[...] = updated * jnp.where(rare_ref[...] == 1, target / norm, 1.0)


def merge(grads, ids, table_t, small, rare, run, ent, reps, cap, group):
    width, rows = table_t.shape
    piece = rows // reps
    vmem = pl.BlockSpec(memory_space=pltpu.VMEM)
    return pl.pallas_call(
        functools.partial(merge_kernel, ent, reps, cap, group),
        out_shape=(jax.ShapeDtypeStruct((width, rows), F32), jax.ShapeDtypeStruct((16, 128), F32)),
        in_specs=[vmem] * 6, out_specs=(vmem,) * 2,
        scratch_shapes=[pltpu.VMEM((ent, cap, width), F32), pltpu.VMEM((reps, width, piece), F32),
                        pltpu.VMEM((reps, width, piece), F32), pltpu.VMEM((width, rows), F32),
                        pltpu.VMEM((3, 16, 128), F32), pltpu.VMEM((reps, 16, 128), F32),
                        pltpu.VMEM((group, 16, 128), F32), pltpu.VMEM((ent // group, 16, 128), F32)]
        + [pltpu.SemaphoreType.DMA] * 12,
        compiler_params=pltpu.CompilerParams(collective_id=1, has_side_effects=True, vmem_limit_bytes=24 << 20),
        name="merge",
    )(grads, ids, table_t, small, rare, run)


def body(entity_table, relation_table, filters, projection, request_owner, request_row, relation_id, rare_flag, running_norm):
    ent, reps = lax.axis_size("ent"), lax.axis_size("rep")
    cap, group = 4, 16
    table_t = entity_table.T
    batch, req = relation_id.shape[0], request_row.shape[0]
    width = table_t.shape[0]
    fetched, ids, slot = fetch(request_owner.reshape(1, req), request_row.reshape(1, req), table_t, ent, cap)
    send, small = compute(fetched.reshape(ent * cap, width), slot, relation_table.T, relation_id.reshape(1, batch),
                          filters, projection.T, projection)
    new_t, total = merge(send.reshape(ent, cap, width), ids, table_t, small, rare_flag.reshape(1, -1),
                         running_norm.reshape(1, 1), ent, reps, cap, group)
    filter_grad = total[:9, :FILT].T / (batch * ent * reps)
    return new_t.T, filter_grad


def solution(mesh):
    in_specs = (P("ent", None), P(), P(), P(), P(("ent", "rep"), None), P(("ent", "rep")), P(("ent", "rep")), P("ent"), P())
    return jax.shard_map(body, mesh=mesh, in_specs=in_specs, out_specs=(P("ent", None), P()), check_vma=False)
```

time: 544 us -> 126 us (0.23)
  blocking collectives: 380 us -> 0 us
  Pallas kernels: 0 us -> 109 us
  matrix products: 46 us -> 0 us
  waiting for transfers between devices: 28 us -> 0 us
  starting transfers between devices: 24.6 us -> 0 us
  other arithmetic: 18.4 us -> 0.6 us
  between operations: 16.1 us -> 1.36 us
  local copies, waits for them, and re-layouts: 25.1 us -> 14.6 us
    psum x2 -> x0, blocking collectives: 345 us -> none  [the longest x1 247 us: body(): norm_total = lax.psum(local_norm, 'ent')]
    pallas_call x0 -> x3, Pallas kernels: none -> 109 us  [the longest x1 47.4 us: merge(): pl.pallas_call(functools.partial(merge_kernel, ent, reps, cap, group), ou...]
    conv_general_dilated x3 -> x0, matrix products: 39.5 us -> none  [conv_act(): lax.conv_general_dilated(stacked, kernel, (1, 1), 'VALID', precision=lax....]
    all_to_all x2 -> x0, waiting for transfers between devices: 28 us -> none  [the longest x1 17.8 us: body(): lax.all_to_all(found_rows, 'ent', split_axis=0, concat_axis=0, tiled=True)]
    all_to_all x1 -> x0, blocking collectives: 26.3 us -> none  [body(): lax.all_to_all(send_grads, 'ent', split_axis=0, concat_axis=0, tiled=True)]
    all_to_all x2 -> x0, starting transfers between devices: 24.1 us -> none  [the longest x1 18.4 us: body(): lax.all_to_all(send_ids, 'ent', split_axis=0, concat_axis=0, tiled=True)]
    scatter-add x1 -> x0, other arithmetic: 12.1 us -> none  [body(): summed_grad = jnp.zeros(entity_table.shape, jnp.float32).at[all_ids.resha...]
    all_gather x1 -> x0, blocking collectives: 8.44 us -> none  [body(): all_ids = lax.all_gather(wanted, 'rep', axis=0, tiled=True)]
  transfers between devices with their start and end apart: 3 -> 0, of which waited for: 2 -> 0; matrix products, arithmetic and copies ran while one was open for 2% -> 0% of each run, Pallas kernels for 0% -> 0%
where the time goes in v1:
time: 126 us; the launch traced here: 125 us
  Pallas kernels  109 us (87%)
  local copies, waits for them, and re-layouts  14.6 us (12%)
  between operations  1.36 us (1%)
    pallas_call x1, Pallas kernels, merge(): pl.pallas_call(functools.partial(merge_kernel, ent, reps, cap, group), ou...  47.4 us
    pallas_call x1, Pallas kernels, fetch(): pl.pallas_call(functools.partial(fetch_kernel, ent, cap), out_shape=(jax....  41.8 us
    pallas_call x1, Pallas kernels, compute(): pl.pallas_call(compute_kernel, out_shape=(jax.ShapeDtypeStruct((slots, wi...  19.4 us
    unnamed x21, local copies, waits for them, and re-layouts  13.5 us

profile of v1, /device:TPU:1, one launch (start us, length us, event | category | flops | bytes accessed | tf_op | source)
XLA Modules:
  0.0 125.2 jit_solution(7708878415100917566)
XLA Ops:
  0.6 0.7 reshape.29.row_ref
  1.3 0.0 copy-start.2
  1.3 1.0 copy-done.2
  2.3 0.0 copy-start.6
  2.3 0.7 copy-done.6
  3.0 41.8 %fetch.1 = (f32[128,4,200]{2,1,0:T(4,128)S(1)}, f32[128,128]{1,0:T(8,128)S(1)}, s32[1,320]{1,0:T(1,128)S(1)}) custom-call(s32[1,320]{1,0:T(1,128)S(1)} %bitcast.19, s32[1,320]{1,0:T(1,128)S(1)} %reshape.29.row_ref, f32[200,512]{1,0:T(8,128)S(1)} %bitcast.14), custom_call_target="tpu_custom_call" | custom-call | tf_op jit(solution)/shard_map/fetch/pallas_call | solution.py:96
  44.9 0.0 copy-start.8
  44.9 0.0 copy-start.4
  44.9 0.0 copy-start.7
  44.9 0.2 reshape.30.fetched_ref
  45.1 6.5 %copy.13 = bf16[9728,200]{1,0:T(8,128)(2,1)} copy(bf16[9728,200]{0,1:T(8,128)(2,1)} %param.12) | data formatting | bytes 7782400 | tf_op args[3]
  51.6 0.0 copy-done.8
  51.6 0.1 copy.14.filt_ref
  51.7 0.0 copy-done.4
  51.7 0.0 copy-done.7
  51.7 0.0 copy-start
  51.7 2.4 %copy-done = bf16[9728,200]{1,0:T(8,128)(2,1)S(1)} copy-done((bf16[9728,200]{1,0:T(8,128)(2,1)S(1)}, bf16[9728,200]{1,0:T(8,128)(2,1)}, u32[]{:S(2)}) %copy-start) | copy-done | bytes 3891224
  54.1 0.0 copy-start.1
  54.1 2.1 %copy-done.1 = bf16[9728,200]{0,1:T(8,128)(2,1)S(1)} copy-done((bf16[9728,200]{0,1:T(8,128)(2,1)S(1)}, bf16[9728,200]{0,1:T(8,128)(2,1)}, u32[]{:S(2)}) %copy-start.1) | copy-done | bytes 3891224
  56.2 0.0 copy-start.3
  56.2 0.0 copy-start.5
  56.2 19.4 %triples.1 = (f32[512,200]{1,0:T(8,128)S(1)}, f32[16,128]{1,0:T(8,128)S(1)}) custom-call(f32[512,200]{1,0:T(8,128)S(1)} %reshape.30.fetched_ref, s32[1,320]{1,0:T(1,128)S(1)} %get-tuple-element.10.slot_ref, bf16[200,822]{1,0:T(8,128)(2,1)S(1)} %bitcast.17, s32[1,128]{1,0:T(1,128)S(1)} %bitcast.20, f32[32,9]{1,0:T(8,128)S(1)} %copy.14.filt_ref, ...), custom_call_target="tpu_custom_call" | custom-call | tf_op jit(solution)/shard_map/triples/pallas_call | solution.py:215
  75.5 0.2 reshape.33.grads_ref
  76.4 0.0 copy-done.3
  76.4 0.0 copy-done.5
  76.4 47.4 %merge.1 = (f32[200,512]{1,0:T(8,128)S(1)}, f32[16,128]{1,0:T(8,128)S(1)}) custom-call(f32[128,4,200]{2,1,0:T(4,128)S(1)} %reshape.33.grads_ref, f32[128,128]{1,0:T(8,128)S(1)} %get-tuple-element.12.ids_ref, f32[200,512]{1,0:T(8,128)S(1)} %bitcast.15, f32[16,128]{1,0:T(8,128)S(1)} %get-tuple-element.13.small_ref, s32[1,512]{1,0:T(1,128)S(1)} %bitcast.18, ...), custom_call_target="tpu_custom_call" | custom-call | tf_op jit(solution)/shard_map/merge/pallas_call | solution.py:313
  123.8 0.6 multiply_bitcast_fusion
  124.4 0.8 copy.17
Async XLA Ops:
  1.3 1.0 copy-start.2
  2.3 0.7 copy-start.6
  44.9 6.7 %copy-start.8 = (f32[32,9]{0,1:T(8,128)S(1)}, f32[32,9]{0,1:T(8,128)}, u32[]{:S(2)}) copy-start(f32[32,9]{0,1:T(8,128)} %param.11) | copy-start | bytes 3460
  44.9 6.8 %copy-start.4 = (bf16[822,200]{0,1:T(8,128)(2,1)S(1)}, bf16[822,200]{0,1:T(8,128)(2,1)}, u32[]{:S(2)}) copy-start(bf16[822,200]{0,1:T(8,128)(2,1)} %param.10) | copy-start | bytes 986404
  44.9 6.8 %copy-start.7 = (s32[128]{0:T(128)S(1)}, s32[128]{0:T(128)}, u32[]{:S(2)}) copy-start(s32[128]{0:T(128)} %param.15) | copy-start | bytes 1540
  51.7 2.4 %copy-start = (bf16[9728,200]{1,0:T(8,128)(2,1)S(1)}, bf16[9728,200]{1,0:T(8,128)(2,1)}, u32[]{:S(2)}) copy-start(bf16[9728,200]{1,0:T(8,128)(2,1)} %copy.13) | copy-start | bytes 11673604
  54.1 2.1 %copy-start.1 = (bf16[9728,200]{0,1:T(8,128)(2,1)S(1)}, bf16[9728,200]{0,1:T(8,128)(2,1)}, u32[]{:S(2)}) copy-start(bf16[9728,200]{0,1:T(8,128)(2,1)} %param.12) | copy-start | bytes 11673604
  56.2 20.2 %copy-start.3 = (f32[512,200]{0,1:T(8,128)S(1)}, f32[512,200]{0,1:T(8,128)}, u32[]{:S(2)}) copy-start(f32[512,200]{0,1:T(8,128)} %param.9) | copy-start | bytes 1228804
  56.2 20.2 %copy-start.5 = (s32[512]{0:T(512)S(1)}, s32[512]{0:T(512)}, u32[]{:S(2)}) copy-start(s32[512]{0:T(512)} %param.16) | copy-start | bytes 6148

commit v2 on v0

v2 whole, which is shorter than its diff:
```python
import functools
import jax
import jax.numpy as jnp
from jax import lax
from jax.experimental import pallas as pl
from jax.experimental.pallas import tpu as pltpu
from jax.sharding import PartitionSpec as P

MESH = pl.DeviceIdType.MESH
HI = lax.Precision.HIGHEST
F32, BF16, I32 = jnp.float32, jnp.bfloat16, jnp.int32
NN = (((1,), (0,)), ((), ()))
NT = (((1,), (1,)), ((), ()))
TN = (((0,), (0,)), ((), ()))
learn_rate, norm_eps = 0.5, 1e-06
FILT, OUT_ROWS, OUT_COLS, IMG_ROWS, IMG_COLS, PITCH = 32, 38, 8, 40, 10, 16
HEAD_ROWS = 20
PAIRS, HEAD_PAIRS = OUT_ROWS // 2, HEAD_ROWS // 2
PER = OUT_ROWS * OUT_COLS
BAND = FILT * 16
CAP, GROUP = 4, 16
NORM_ROW = 9


def iota(shape, dim):
    return lax.broadcasted_iota(I32, shape, dim)


def mm(a, b, dims=NN):
    return lax.dot_general(a, b, dims, preferred_element_type=F32)


def mm_hi(a, b, dims=NN):
    return lax.dot_general(a, b, dims, precision=HI, preferred_element_type=F32)


def split(v):
    high = v.astype(BF16)
    return high, (v - high.astype(F32)).astype(BF16)


def one(mask):
    return mask.astype(F32).astype(BF16)


def sigmoid(v):
    return 0.5 * jnp.tanh(0.5 * v) + 0.5


def band_matrix(filt):
    r, k = iota((16, 64), 0), iota((16, 64), 1)
    di, dj = k // PITCH - r // OUT_COLS, k % PITCH - r % OUT_COLS
    total = jnp.zeros((FILT, 16, 64), F32)
    for t in range(9):
        mask = ((di == t // 3) & (dj == t % 3)).astype(F32)
        total = total + filt[:, t : t + 1][:, :, None] * mask[None]
    return total.reshape(BAND, 64)


def fill_image(img, base, strip, rows):
    for r in range(rows):
        img[pl.ds(PITCH * (base + r), IMG_COLS), :] = strip[pl.ds(IMG_COLS * r, IMG_COLS), :]


def step_kernel(ent, reps, *refs):
    (owner_h, row_h, relid_h, rare_h, run_ref, table_h, rel_h, filt_h, projt_h, out_ref, total_ref,
     owner_v, row_v, relid_v, rare_v, table_v, rel_v, filt_v, projt_v,
     proj_v, send1, got1, send2, got2, found, fetched, outgoing, land,
     val, strip, img, hi_img, lo_img, lhs_v, bandt_v, feat, dact, left_v, dimg, acc_v, turn,
     part, pland, upd, s_here, s_x, s_g, s_y, load, dma) = refs
    me, rep = lax.axis_index("ent"), lax.axis_index("rep")
    width, rows = table_v.shape
    req, batch, rels = owner_v.shape[1], relid_v.shape[0], rel_v.shape[1]
    neg = req - 2 * batch
    slots, piece, outer = ent * CAP, rows // reps, ent // GROUP
    y, g = me // GROUP, me % GROUP
    barrier = pltpu.get_barrier_semaphore()

    def loop(start, stop, step):
        lax.fori_loop(start, stop, lambda i, c: (step(i), c)[1], 0)

    def remote(src, dst, which, p, r):
        pltpu.make_async_remote_copy(src_ref=src, dst_ref=dst, send_sem=dma.at[2 * which], recv_sem=dma.at[2 * which + 1],
                                     device_id=(p, r), device_id_type=MESH).start()

    def drain(ref, count, which, side):
        at = ref.at[pl.ds(0, count)]
        pltpu.make_async_copy(at, at, dma.at[2 * which + side]).wait()

    def greet(p, r):
        pl.semaphore_signal(barrier, inc=1, device_id=(p, r), device_id_type=MESH)

    def in_group(i):
        return y * GROUP + (g + i) % GROUP

    def in_outer(i):
        return (y + i) % outer * GROUP + g

    loop(1, GROUP, lambda i: greet(in_group(i), rep))
    loop(1, outer, lambda i: greet(in_outer(i), rep))
    loop(1, reps, lambda i: greet(me, (rep + i) % reps))
    loads = [pltpu.make_async_copy(a, b, load.at[i]) for i, (a, b) in enumerate(
        [(owner_h, owner_v), (row_h, row_v), (table_h, table_v), (filt_h, filt_v), (relid_h, relid_v), (rel_h, rel_v),
         (projt_h, projt_v), (rare_h, rare_v)])]
    for copy in loads:
        copy.start()

    loads[0].wait()
    loads[1].wait()
    owner = owner_v[...]
    place = owner % GROUP * outer + owner // GROUP
    named = iota((ent, req), 0) == place
    before = one(iota((req, req), 0) < iota((req, req), 1))
    rank = jnp.sum(jnp.where(named, mm(one(named), before), 0.0), 0, keepdims=True).astype(I32)
    slot = owner * CAP + rank
    marked = jnp.where(iota((128, req), 0) == rank + g * CAP, row_v[...].reshape(1, req).astype(F32), 0.0)
    send1[...] = mm_hi(named.astype(F32), marked, NT).reshape(GROUP, outer, 128)
    got1[pl.ds(g, 1)] = send1[pl.ds(g, 1)]
    pl.semaphore_wait(barrier, GROUP + outer + reps - 3)
    loop(1, GROUP, lambda i: remote(send1.at[(g + i) % GROUP], got1.at[g], 0, in_group(i), rep))
    loads[2].wait()
    loads[3].wait()
    table_high, table_low = split(table_v[...])
    band = band_matrix(filt_v[...])
    band_high, band_low = split(band)
    lhs_v[...] = jnp.concatenate([band_high, band_high, band_low], 1)
    bandt_v[...] = jnp.concatenate([band, band - band_high.astype(F32)], 1).T.astype(BF16)
    drain(got1, GROUP - 1, 0, 1)
    send2[...] = jnp.sum(got1[...], 0).reshape(outer, 1, 128)
    got2[pl.ds(y, 1)] = send2[pl.ds(y, 1)]
    loop(1, outer, lambda i: remote(send2.at[(y + i) % outer], got2.at[y], 1, in_outer(i), rep))
    loads[4].wait()
    loads[5].wait()
    img[...] = jnp.zeros(img.shape, F32)
    strip[...] = mm(rel_v[...], one(iota((rels, batch), 0) == relid_v[...].reshape(1, batch)))
    fill_image(img, HEAD_ROWS, strip, HEAD_ROWS)
    drain(got2, outer - 1, 1, 1)
    spread = mm_hi((iota((slots, outer), 0) // (GROUP * CAP) == iota((slots, outer), 1)).astype(F32),
                   got2[...].reshape(outer, 128))
    keep = iota((slots, 128), 0) % (GROUP * CAP) == iota((slots, 128), 1)
    wanted = jnp.sum(jnp.where(keep, spread, 0.0), 1, keepdims=True)
    hot_rows = one(iota((slots, rows), 1).astype(F32) == wanted)
    picked = mm(hot_rows, table_high, NT) + mm(hot_rows, table_low, NT)
    found[...] = picked.reshape(ent, CAP, width)
    loop(1, ent, lambda i: remote(found.at[(me + i) % ent], fetched.at[me], 2, (me + i) % ent, rep))
    fetched[pl.ds(me, 1)] = found[pl.ds(me, 1)]

    loads[6].wait()

    def turn_over(i, c):
        at = pl.ds(pl.multiple_of(i * 512, 512), 512)
        proj_v[at, :] = projt_v[:, at].T
        return c

    lax.fori_loop(0, FILT * PER // 512, turn_over, 0)
    rel_at = pl.ds(HEAD_ROWS * PITCH, HEAD_ROWS * PITCH)
    hi_img[rel_at, :] = img[rel_at, :].astype(BF16)
    lo_img[rel_at, :] = jnp.zeros((HEAD_ROWS * PITCH, batch), BF16)

    def conv(q):
        at = pl.ds(pl.multiple_of(q * 2 * PITCH, 2 * PITCH), 4 * PITCH)
        hi, lo = hi_img[at, :], lo_img[at, :]
        v = mm(lhs_v[...], jnp.concatenate([hi, lo, hi], 0))
        s = sigmoid(v)
        a = v * s
        out = pl.ds(pl.multiple_of(q * 16, 16), 16)
        feat[:, out, :] = a.astype(BF16).reshape(FILT, 16, batch)
        dact[:, out, :] = (s + a * (1.0 - s)).reshape(FILT, 16, batch)

    loop(HEAD_PAIRS, PAIRS, conv)
    drain(fetched, ent - 1, 2, 1)

    hot = one(iota((slots, req), 0) == slot)
    high, low = split(fetched[...].reshape(slots, width))
    val[...] = mm(high, hot, TN) + mm(low, hot, TN)
    strip[...] = val[:, pl.ds(0, batch)]
    fill_image(img, 0, strip, HEAD_ROWS)
    head_at = pl.ds(0, HEAD_ROWS * PITCH)
    high, low = split(img[head_at, :])
    hi_img[head_at, :] = high
    lo_img[head_at, :] = low
    for q in range(HEAD_PAIRS):
        conv(q)
    projected = mm(projt_v[...], feat[...].reshape(FILT * PER, batch))
    sig = sigmoid(projected)
    hidden = projected * sig
    pos, negs = val[:, pl.ds(batch, batch)], val[:, pl.ds(2 * batch, neg)]
    score_pos = jnp.sum(hidden * pos, 0, keepdims=True)
    score_neg = mm_hi(negs, hidden, TN)
    grad_pos = -sigmoid(-score_pos)
    grad_neg = sigmoid(score_neg) / neg
    grad_hidden = grad_pos * pos + mm_hi(negs, grad_neg)
    grad_proj = (grad_hidden * sig * (1.0 + projected * (1.0 - sig))).astype(BF16)
    val[:, pl.ds(batch, batch)] = grad_pos * hidden
    val[:, pl.ds(2 * batch, neg)] = mm_hi(hidden, grad_neg, NT)
    dimg[...] = jnp.zeros(dimg.shape, F32)

    def back(q):
        out = pl.ds(pl.multiple_of(q * 16, 16), 16)
        turned = proj_v.reshape(FILT, PER, width)[:, out, :].reshape(BAND, width)
        d = mm(turned, grad_proj) * dact[:, out, :].reshape(BAND, batch)
        return split(d)

    for q in range(HEAD_PAIRS):
        dh, dl = back(q)
        left_v[q] = jnp.concatenate([dh, dl], 1)
        both = mm(bandt_v[...], dh)
        at = pl.ds(q * 2 * PITCH, 4 * PITCH)
        dimg[at, :] += both[:64] + both[64:] + mm(bandt_v[pl.ds(0, 64), :], dl)
    for r in range(HEAD_ROWS):
        strip[pl.ds(IMG_COLS * r, IMG_COLS), :] = dimg[pl.ds(PITCH * r, IMG_COLS), :]
    val[:, pl.ds(0, batch)] = strip[...]
    high, low = split(val[...])
    outgoing[...] = (mm(hot, high, NT) + mm(hot, low, NT)).reshape(ent, CAP, width)
    loop(1, ent, lambda i: remote(outgoing.at[(me + i) % ent], land.at[me], 3, (me + i) % ent, rep))
    land[pl.ds(me, 1)] = outgoing[pl.ds(me, 1)]

    acc_v[...] = jnp.zeros(acc_v.shape, F32)

    def add_filter(q, left):
        at = pl.ds(pl.multiple_of(q * 2 * PITCH, 2 * PITCH), 4 * PITCH)
        hi, lo = hi_img[at, :], lo_img[at, :]
        right = jnp.concatenate([jnp.concatenate([hi, hi], 1), jnp.concatenate([lo, jnp.zeros_like(lo)], 1)], 0)
        acc_v[...] += mm(left, right, NT)

    loop(0, HEAD_PAIRS, lambda q: add_filter(q, left_v[q]))
    loop(HEAD_PAIRS, PAIRS, lambda q: add_filter(q, jnp.concatenate(back(q), 1)))
    both = acc_v[...]
    acc_v[...] = both + pltpu.roll(both, 64, 1)
    taps = acc_v[pl.ds(0, FILT, stride=16), :]
    for k in range(1, 16):
        shift = k // OUT_COLS * PITCH + k % OUT_COLS
        taps = taps + pltpu.roll(acc_v[pl.ds(k, FILT, stride=16), :], 128 - shift, 1)
    turn[...] = jnp.concatenate([taps, jnp.zeros((128 - FILT, 128), F32)], 0).T
    filter_part = jnp.concatenate([turn[pl.ds(PITCH * i, 3), :] for i in range(3)] + [jnp.zeros((7, 128), F32)], 0)
    drain(land, ent - 1, 3, 1)

    high, low = split(land[...].reshape(slots, width))
    sums = mm(high, hot_rows, TN) + mm(low, hot_rows, TN)

    def columns(r):
        return pl.ds(pl.multiple_of(r * piece, piece), piece)

    for r in range(reps):
        part[r] = sums[:, r * piece : (r + 1) * piece]
    pland[pl.ds(rep, 1)] = part[pl.ds(rep, 1)]
    loop(1, reps, lambda i: remote(part.at[(rep + i) % reps], pland.at[rep], 4, me, (rep + i) % reps))
    drain(pland, reps - 1, 4, 1)
    block = table_v[:, columns(rep)] - learn_rate * jnp.sum(pland[...], 0)
    upd[:, columns(rep)] = block
    mine = upd.at[:, columns(rep)]
    norms = jnp.sqrt(jnp.sum(block * block, 0, keepdims=True) + norm_eps)
    here = jnp.where(iota((16, piece), 0) == NORM_ROW, norms, filter_part)
    s_here[0] = here
    s_x[pl.ds(rep, 1)] = here[None]
    loop(1, reps, lambda i: remote(s_here.at[0], s_x.at[rep], 5, me, (rep + i) % reps))
    loop(1, reps, lambda i: remote(mine, upd.at[:, columns(rep)], 8, me, (rep + i) % reps))
    drain(s_x, reps - 1, 5, 1)
    s_here[1] = jnp.sum(s_x[...], 0)
    s_g[pl.ds(g, 1)] = s_here[pl.ds(1, 1)]
    loop(1, GROUP, lambda i: remote(s_here.at[1], s_g.at[g], 6, in_group(i), rep))
    drain(s_g, GROUP - 1, 6, 1)
    s_here[2] = jnp.sum(s_g[...], 0)
    s_y[pl.ds(y, 1)] = s_here[pl.ds(2, 1)]
    loop(1, outer, lambda i: remote(s_here.at[2], s_y.at[y], 7, in_outer(i), rep))
    loads[7].wait()
    drain(send1, GROUP - 1, 0, 0)
    drain(send2, outer - 1, 1, 0)
    drain(found, ent - 1, 2, 0)
    drain(outgoing, ent - 1, 3, 0)
    drain(part, reps - 1, 4, 0)
    drain(s_x, reps - 1, 5, 0)
    drain(s_g, GROUP - 1, 6, 0)
    drain(s_y, outer - 1, 7, 1)
    drain(s_y, outer - 1, 7, 0)
    total = jnp.sum(s_y[...], 0)
    total_ref[...] = total
    norm_total = jnp.sum(total[NORM_ROW : NORM_ROW + 1, :], 1, keepdims=True)
    target = 0.25 * run_ref[...] + 0.75 * norm_total / (rows * ent)
    three = upd.at[:, pl.ds(0, (reps - 1) * piece)]
    pltpu.make_async_copy(three, three, dma.at[16]).wait()
    pltpu.make_async_copy(three, three, dma.at[17]).wait()
    updated = upd[...]
    norm = jnp.sqrt(jnp.sum(updated * updated, 0, keepdims=True) + norm_eps)
    out_ref[...] = updated * jnp.where(rare_v[...].reshape(1, rows) == 1, target / norm, 1.0)


def step(owner, row, relid, rare, run, table_t, rel_t, filt, proj_t, ent, reps):
    width, rows = table_t.shape
    req, batch, feats = owner.shape[1], relid.shape[0], proj_t.shape[1]
    piece, outer = rows // reps, ent // GROUP
    vmem, hbm = pl.BlockSpec(memory_space=pltpu.VMEM), pl.BlockSpec(memory_space=pltpu.HBM)
    v = pltpu.VMEM
    exchange = v((ent, CAP, width), F32)
    return pl.pallas_call(
        functools.partial(step_kernel, ent, reps),
        out_shape=(jax.ShapeDtypeStruct((width, rows), F32), jax.ShapeDtypeStruct((16, 128), F32)),
        in_specs=[hbm] * 4 + [vmem] + [hbm] * 4, out_specs=(vmem,) * 2,
        scratch_shapes=[
            v(owner.shape, I32), v(row.shape, I32), v(relid.shape, I32), v(rare.shape, I32), v((width, rows), F32),
            v(rel_t.shape, BF16), v(filt.shape, F32), v(proj_t.shape, BF16),
            v((feats, width), BF16), v((GROUP, outer, 128), F32), v((GROUP, outer, 128), F32), v((outer, 1, 128), F32),
            v((outer, 1, 128), F32), exchange, exchange, exchange, exchange,
            v((width, req), F32), v((width, batch), F32), v((IMG_ROWS * PITCH, batch), F32),
            v((IMG_ROWS * PITCH, batch), BF16), v((IMG_ROWS * PITCH, batch), BF16), v((BAND, 192), BF16),
            v((128, BAND), BF16), v((FILT, PER, batch), BF16), v((FILT, PER, batch), F32),
            v((HEAD_PAIRS, BAND, 2 * batch), BF16), v(((HEAD_ROWS + 2) * PITCH, batch), F32), v((BAND, 128), F32),
            v((128, 128), F32),
            v((reps, width, piece), F32), v((reps, width, piece), F32), v((width, rows), F32), v((3, 16, 128), F32),
            v((reps, 16, 128), F32), v((GROUP, 16, 128), F32), v((outer, 16, 128), F32),
            pltpu.SemaphoreType.DMA((8,)), pltpu.SemaphoreType.DMA((18,))],
        compiler_params=pltpu.CompilerParams(collective_id=0, has_side_effects=True, vmem_limit_bytes=60 << 20),
        name="step",
    )(owner, row, relid, rare, run, table_t, rel_t, filt, proj_t)


def body(entity_table, relation_table, filters, projection, request_owner, request_row, relation_id, rare_flag, running_norm):
    ent, reps = lax.axis_size("ent"), lax.axis_size("rep")
    batch, req = relation_id.shape[0], request_row.shape[0]
    new_t, total = step(request_owner.reshape(1, req), request_row, relation_id, rare_flag, running_norm.reshape(1, 1),
                        entity_table.T, relation_table.T, filters, projection.T, ent, reps)
    filter_grad = total[:9, :FILT].T / (batch * ent * reps)
    return new_t.T, filter_grad


def solution(mesh):
    in_specs = (P("ent", None), P(), P(), P(), P(("ent", "rep"), None), P(("ent", "rep")), P(("ent", "rep")), P("ent"), P())
    return jax.shard_map(body, mesh=mesh, in_specs=in_specs, out_specs=(P("ent", None), P()), check_vma=False)
```

time: 544 us -> 93.6 us (0.17); the launches traced: 538 us -> 93.3 us
  blocking collectives: 380 us -> 0 us
  Pallas kernels: 0 us -> 87.6 us
  matrix products: 46 us -> 0 us
  waiting for transfers between devices: 28 us -> 0 us
  starting transfers between devices: 24.6 us -> 0 us
  local copies, waits for them, and re-layouts: 25.1 us -> 3.16 us
  other arithmetic: 18.4 us -> 1.3 us
  between operations: 16.1 us -> 1.29 us
    psum x2 -> x0, blocking collectives: 345 us -> none  [the longest x1 247 us: body(): norm_total = lax.psum(local_norm, 'ent')]
    pallas_call x0 -> x1, Pallas kernels: none -> 87.6 us  [step(): pl.pallas_call(functools.partial(step_kernel, ent, reps), out_shape=(jax....]
    conv_general_dilated x3 -> x0, matrix products: 39.5 us -> none  [conv_act(): lax.conv_general_dilated(stacked, kernel, (1, 1), 'VALID', precision=lax....]
    all_to_all x2 -> x0, waiting for transfers between devices: 28 us -> none  [the longest x1 17.8 us: body(): lax.all_to_all(found_rows, 'ent', split_axis=0, concat_axis=0, tiled=True)]
    all_to_all x1 -> x0, blocking collectives: 26.3 us -> none  [body(): lax.all_to_all(send_grads, 'ent', split_axis=0, concat_axis=0, tiled=True)]
    all_to_all x2 -> x0, starting transfers between devices: 24.1 us -> none  [the longest x1 18.4 us: body(): lax.all_to_all(send_ids, 'ent', split_axis=0, concat_axis=0, tiled=True)]
    scatter-add x1 -> x0, other arithmetic: 12.1 us -> none  [body(): summed_grad = jnp.zeros(entity_table.shape, jnp.float32).at[all_ids.resha...]
    all_gather x1 -> x0, blocking collectives: 8.44 us -> none  [body(): all_ids = lax.all_gather(wanted, 'rep', axis=0, tiled=True)]
  transfers between devices with their start and end apart: 3 -> 0, of which waited for: 2 -> 0; matrix products, arithmetic and copies ran while one was open for 2% -> 0% of each run, Pallas kernels for 0% -> 0%
where the time goes in v2:
time: 93.6 us; the launch traced here: 93.3 us
  Pallas kernels  87.6 us (94%)
  local copies, waits for them, and re-layouts  3.16 us (3%)
  other arithmetic  1.3 us (1%)
  between operations  1.29 us (1%)
    pallas_call x1, Pallas kernels, step(): pl.pallas_call(functools.partial(step_kernel, ent, reps), out_shape=(jax....  87.6 us
    unnamed x2, local copies, waits for them, and re-layouts  3.16 us

profile of v2, /device:TPU:1, one launch (start us, length us, event | category | flops | bytes accessed | tf_op | source)
XLA Modules:
  0.0 93.3 jit_solution(8566307512874558530)
XLA Ops:
  1.3 1.4 %copy.11.refs_7_ = f32[32,9]{1,0:T(8,128)} copy(f32[32,9]{0,1:T(8,128)} %param.11) | data formatting | bytes 2304 | tf_op args[2]
  2.7 87.6 %step.1 = (f32[200,512]{1,0:T(8,128)}, f32[16,128]{1,0:T(8,128)}) custom-call(s32[1,320]{1,0:T(1,128)} %bitcast.13, s32[320]{0:T(512)} %refs_1_.1, s32[128]{0:T(128)} %refs_2_.1, s32[512]{0:T(512)} %refs_3_.1, f32[1,1]{1,0:T(1,128)} %bitcast.8.refs_4_, f32[200,512]{1,0:T(8,128)} %bitcast.10, bf16[200,822]{1,0:T(8,128)(2,1)} %bitcast.12, ...), custom_call_target="tpu_custom_call" | custom-call | tf_op jit(solution)/shard_map/step/pallas_call | solution.py:295
  90.2 1.3 %multiply_bitcast_fusion = f32[32,9]{0,1:T(8,128)} fusion(f32[16,128]{1,0:T(8,128)} %get-tuple-element.5), kind=kLoop, calls=%fused_computation | loop fusion | flops 288 | bytes 2304 | tf_op jit(solution)/shard_map/div | solution.py:322
  91.5 1.8 %copy.14 = f32[512,200]{0,1:T(8,128)} copy(f32[512,200]{0,1:T(8,128)} %bitcast.11) | data formatting | bytes 819200

commit v3 on v2

--- a/solution.py
+++ b/solution.py
@@ -19,7 +19,6 @@
 PER = OUT_ROWS * OUT_COLS
 BAND = FILT * 16
 CAP, GROUP = 4, 16
-NORM_ROW = 9
 
 
 def iota(shape, dim):
@@ -57,6 +56,19 @@
     return total.reshape(BAND, 64)
 
 
+def pack_tail(t, ent, tail):
+    lane = iota((ent, 128), 1)
+    t0, t1, t2, t3 = [t[i * ent : (i + 1) * ent] for i in range(CAP)]
+    return (jnp.where(lane < tail, t0, pltpu.roll(t3, tail, 1)),
+            jnp.where(lane < tail, t1, pltpu.roll(t3, 2 * tail - 128, 1)), t2)
+
+
+def unpack_tail(r0, r1, r2, tail):
+    lane = iota(r0.shape, 1)
+    t3 = jnp.where(lane < 128 - tail, pltpu.roll(r0, 128 - tail, 1), pltpu.roll(r1, 256 - 2 * tail, 1))
+    return jnp.concatenate([r0, r1, r2, t3], 0)
+
+
 def fill_image(img, base, strip, rows):
     for r in range(rows):
         img[pl.ds(PITCH * (base + r), IMG_COLS), :] = strip[pl.ds(IMG_COLS * r, IMG_COLS), :]
@@ -65,15 +77,16 @@
 def step_kernel(ent, reps, *refs):
     (owner_h, row_h, relid_h, rare_h, run_ref, table_h, rel_h, filt_h, projt_h, out_ref, total_ref,
      owner_v, row_v, relid_v, rare_v, table_v, rel_v, filt_v, projt_v,
-     proj_v, send1, got1, send2, got2, found, fetched, outgoing, land,
+     proj_v, send1, got1, send2, got2, found, fetched, out_a, out_b, land_a, land_b,
      val, strip, img, hi_img, lo_img, lhs_v, bandt_v, feat, dact, left_v, dimg, acc_v, turn,
-     part, pland, upd, s_here, s_x, s_g, s_y, load, dma) = refs
+     part_a, part_b, pland_a, pland_b, upd, f_here, f_x, f_g, f_y, n_here, n_a, n_b, load, dma) = refs
     me, rep = lax.axis_index("ent"), lax.axis_index("rep")
     width, rows = table_v.shape
     req, batch, rels = owner_v.shape[1], relid_v.shape[0], rel_v.shape[1]
     neg = req - 2 * batch
     slots, piece, outer = ent * CAP, rows // reps, ent // GROUP
     y, g = me // GROUP, me % GROUP
+    tail, half = width - 128, width // 16 * 8 + 8
     barrier = pltpu.get_barrier_semaphore()
 
     def loop(start, stop, step):
@@ -108,40 +121,54 @@
     loads[0].wait()
     loads[1].wait()
     owner = owner_v[...]
-    place = owner % GROUP * outer + owner // GROUP
-    named = iota((ent, req), 0) == place
+    named = one(iota((ent, req), 0) == owner)
     before = one(iota((req, req), 0) < iota((req, req), 1))
-    rank = jnp.sum(jnp.where(named, mm(one(named), before), 0.0), 0, keepdims=True).astype(I32)
-    slot = owner * CAP + rank
-    marked = jnp.where(iota((128, req), 0) == rank + g * CAP, row_v[...].reshape(1, req).astype(F32), 0.0)
-    send1[...] = mm_hi(named.astype(F32), marked, NT).reshape(GROUP, outer, 128)
-    got1[pl.ds(g, 1)] = send1[pl.ds(g, 1)]
+    rank = jnp.sum(named.astype(F32) * mm(named, before), 0, keepdims=True).astype(I32)
+    slot = rank * ent + owner
+    spot = owner % GROUP * (outer * CAP) + y * CAP + rank
+    wide = GROUP * outer * CAP
+    high, low = split(jnp.where(iota((wide, req), 0) == spot, row_v[...].reshape(1, req).astype(F32), 0.0))
+    heard = one(iota((outer, req), 0) == owner // GROUP)
+    ids = mm(heard, high, NT) + mm(heard, low, NT)
+    for j in range(wide // 128):
+        send1[:, j, :] = ids[:, j * 128 : (j + 1) * 128]
+    got1[pl.ds(y, 1)] = send1[pl.ds(y, 1)]
     pl.semaphore_wait(barrier, GROUP + outer + reps - 3)
-    loop(1, GROUP, lambda i: remote(send1.at[(g + i) % GROUP], got1.at[g], 0, in_group(i), rep))
+    loop(1, outer, lambda i: remote(send1.at[(y + i) % outer], got1.at[y], 0, in_outer(i), rep))
     loads[2].wait()
     loads[3].wait()
     table_high, table_low = split(table_v[...])
-    band = band_matrix(filt_v[...])
+    band = band_matrix(filt_v[...].T)
     band_high, band_low = split(band)
     lhs_v[...] = jnp.concatenate([band_high, band_high, band_low], 1)
     bandt_v[...] = jnp.concatenate([band, band - band_high.astype(F32)], 1).T.astype(BF16)
-    drain(got1, GROUP - 1, 0, 1)
-    send2[...] = jnp.sum(got1[...], 0).reshape(outer, 1, 128)
-    got2[pl.ds(y, 1)] = send2[pl.ds(y, 1)]
-    loop(1, outer, lambda i: remote(send2.at[(y + i) % outer], got2.at[y], 1, in_outer(i), rep))
+    drain(got1, outer - 1, 0, 1)
+    send2[...] = jnp.sum(got1[...], 0).reshape(wide // 128, 1, 128)
+    share = GROUP * 128 // wide
+    got2[pl.ds(g, 1)] = send2[pl.ds(g // share, 1)]
+    loop(1, GROUP, lambda i: remote(send2.at[(g + i) % GROUP // share], got2.at[g], 1, in_group(i), rep))
     loads[4].wait()
     loads[5].wait()
     img[...] = jnp.zeros(img.shape, F32)
     strip[...] = mm(rel_v[...], one(iota((rels, batch), 0) == relid_v[...].reshape(1, batch)))
     fill_image(img, HEAD_ROWS, strip, HEAD_ROWS)
-    drain(got2, outer - 1, 1, 1)
-    spread = mm_hi((iota((slots, outer), 0) // (GROUP * CAP) == iota((slots, outer), 1)).astype(F32),
-                   got2[...].reshape(outer, 128))
-    keep = iota((slots, 128), 0) % (GROUP * CAP) == iota((slots, 128), 1)
+    drain(got2, GROUP - 1, 1, 1)
+    src = iota((slots, GROUP), 0) % ent
+    pick = one(src % GROUP == iota((slots, GROUP), 1))
+    high, low = split(got2[...].reshape(GROUP, 128))
+    spread = mm(pick, high) + mm(pick, low)
+    at = iota((slots, 128), 0)
+    keep = g % share * (outer * CAP) + at % ent // GROUP * CAP + at // ent == iota((slots, 128), 1)
     wanted = jnp.sum(jnp.where(keep, spread, 0.0), 1, keepdims=True)
     hot_rows = one(iota((slots, rows), 1).astype(F32) == wanted)
-    picked = mm(hot_rows, table_high, NT) + mm(hot_rows, table_low, NT)
-    found[...] = picked.reshape(ent, CAP, width)
+    picked = mm(hot_rows, table_high[:128], NT) + mm(hot_rows, table_low[:128], NT)
+    for j in range(CAP):
+        found[:, j, :] = picked[j * ent : (j + 1) * ent]
+    blank = jnp.zeros((128 - tail, rows), BF16)
+    picked = (mm(hot_rows, jnp.concatenate([table_high[128:], blank], 0), NT)
+              + mm(hot_rows, jnp.concatenate([table_low[128:], blank], 0), NT))
+    for j, piece_of in enumerate(pack_tail(picked, ent, tail)):
+        found[:, CAP + j, :] = piece_of
     loop(1, ent, lambda i: remote(found.at[(me + i) % ent], fetched.at[me], 2, (me + i) % ent, rep))
     fetched[pl.ds(me, 1)] = found[pl.ds(me, 1)]
 
@@ -171,8 +198,10 @@
     drain(fetched, ent - 1, 2, 1)
 
     hot = one(iota((slots, req), 0) == slot)
-    high, low = split(fetched[...].reshape(slots, width))
-    val[...] = mm(high, hot, TN) + mm(low, hot, TN)
+    high, low = split(jnp.concatenate([fetched[:, j, :] for j in range(CAP)], 0))
+    val[pl.ds(0, 128), :] = mm(high, hot, TN) + mm(low, hot, TN)
+    high, low = split(unpack_tail(fetched[:, CAP, :], fetched[:, CAP + 1, :], fetched[:, CAP + 2, :], tail))
+    val[pl.ds(128, tail), :] = (mm(high, hot, TN) + mm(low, hot, TN))[:tail]
     strip[...] = val[:, pl.ds(0, batch)]
     fill_image(img, 0, strip, HEAD_ROWS)
     head_at = pl.ds(0, HEAD_ROWS * PITCH)
@@ -211,9 +240,18 @@
         strip[pl.ds(IMG_COLS * r, IMG_COLS), :] = dimg[pl.ds(PITCH * r, IMG_COLS), :]
     val[:, pl.ds(0, batch)] = strip[...]
     high, low = split(val[...])
-    outgoing[...] = (mm(hot, high, NT) + mm(hot, low, NT)).reshape(ent, CAP, width)
-    loop(1, ent, lambda i: remote(outgoing.at[(me + i) % ent], land.at[me], 3, (me + i) % ent, rep))
-    land[pl.ds(me, 1)] = outgoing[pl.ds(me, 1)]
+    packed = mm(hot, high[:128], NT) + mm(hot, low[:128], NT)
+    for j in range(CAP):
+        out_a[:, j, :] = packed[j * ent : (j + 1) * ent]
+    loop(1, ent, lambda i: remote(out_a.at[(me + i) % ent], land_a.at[me], 3, (me + i) % ent, rep))
+    blank = jnp.zeros((128 - tail, req), BF16)
+    packed = (mm(hot, jnp.concatenate([high[128:], blank], 0), NT)
+              + mm(hot, jnp.concatenate([low[128:], blank], 0), NT))
+    for j, piece_of in enumerate(pack_tail(packed, ent, tail)):
+        out_b[:, j, :] = piece_of
+    loop(1, ent, lambda i: remote(out_b.at[(me + i) % ent], land_b.at[me], 11, (me + i) % ent, rep))
+    land_a[pl.ds(me, 1)] = out_a[pl.ds(me, 1)]
+    land_b[pl.ds(me, 1)] = out_b[pl.ds(me, 1)]
 
     acc_v[...] = jnp.zeros(acc_v.shape, F32)
 
@@ -233,55 +271,88 @@
         taps = taps + pltpu.roll(acc_v[pl.ds(k, FILT, stride=16), :], 128 - shift, 1)
     turn[...] = jnp.concatenate([taps, jnp.zeros((128 - FILT, 128), F32)], 0).T
     filter_part = jnp.concatenate([turn[pl.ds(PITCH * i, 3), :] for i in range(3)] + [jnp.zeros((7, 128), F32)], 0)
-    drain(land, ent - 1, 3, 1)
-
-    high, low = split(land[...].reshape(slots, width))
-    sums = mm(high, hot_rows, TN) + mm(low, hot_rows, TN)
+    f_here[0] = filter_part
+    f_x[pl.ds(rep, 1)] = filter_part[None]
+    loop(1, reps, lambda i: remote(f_here.at[0], f_x.at[rep], 5, me, (rep + i) % reps))
+    drain(land_a, ent - 1, 3, 1)
+
+    def share_out(sums, here, there, which):
+        for r in range(reps):
+            here[r] = sums[:, r * piece : (r + 1) * piece]
+        there[pl.ds(rep, 1)] = here[pl.ds(rep, 1)]
+        loop(1, reps, lambda i: remote(here.at[(rep + i) % reps], there.at[rep], which, me, (rep + i) % reps))
 
     def columns(r):
         return pl.ds(pl.multiple_of(r * piece, piece), piece)
 
-    for r in range(reps):
-        part[r] = sums[:, r * piece : (r + 1) * piece]
-    pland[pl.ds(rep, 1)] = part[pl.ds(rep, 1)]
-    loop(1, reps, lambda i: remote(part.at[(rep + i) % reps], pland.at[rep], 4, me, (rep + i) % reps))
-    drain(pland, reps - 1, 4, 1)
-    block = table_v[:, columns(rep)] - learn_rate * jnp.sum(pland[...], 0)
+    high, low = split(jnp.concatenate([land_a[:, j, :] for j in range(CAP)], 0))
+    share_out(mm(high, hot_rows, TN) + mm(low, hot_rows, TN), part_a, pland_a, 4)
+    drain(land_b, ent - 1, 11, 1)
+    high, low = split(unpack_tail(land_b[:, 0, :], land_b[:, 1, :], land_b[:, 2, :], tail))
+    share_out((mm(high, hot_rows, TN) + mm(low, hot_rows, TN))[:tail], part_b, pland_b, 12)
+    drain(f_x, reps - 1, 5, 1)
+    f_here[1] = jnp.sum(f_x[...], 0)
+    f_g[pl.ds(g, 1)] = f_here[pl.ds(1, 1)]
+    loop(1, GROUP, lambda i: remote(f_here.at[1], f_g.at[g], 6, in_group(i), rep))
+    drain(pland_a, reps - 1, 4, 1)
+    drain(pland_b, reps - 1, 12, 1)
+    block = table_v[:, columns(rep)] - learn_rate * jnp.concatenate([jnp.sum(pland_a[...], 0), jnp.sum(pland_b[...], 0)], 0)
+    n_here[0] = jnp.sqrt(jnp.sum(block * block, 0, keepdims=True) + norm_eps)
     upd[:, columns(rep)] = block
-    mine = upd.at[:, columns(rep)]
-    norms = jnp.sqrt(jnp.sum(block * block, 0, keepdims=True) + norm_eps)
-    here = jnp.where(iota((16, piece), 0) == NORM_ROW, norms, filter_part)
-    s_here[0] = here
-    s_x[pl.ds(rep, 1)] = here[None]
-    loop(1, reps, lambda i: remote(s_here.at[0], s_x.at[rep], 5, me, (rep + i) % reps))
-    loop(1, reps, lambda i: remote(mine, upd.at[:, columns(rep)], 8, me, (rep + i) % reps))
-    drain(s_x, reps - 1, 5, 1)
-    s_here[1] = jnp.sum(s_x[...], 0)
-    s_g[pl.ds(g, 1)] = s_here[pl.ds(1, 1)]
-    loop(1, GROUP, lambda i: remote(s_here.at[1], s_g.at[g], 6, in_group(i), rep))
-    drain(s_g, GROUP - 1, 6, 1)
-    s_here[2] = jnp.sum(s_g[...], 0)
-    s_y[pl.ds(y, 1)] = s_here[pl.ds(2, 1)]
-    loop(1, outer, lambda i: remote(s_here.at[2], s_y.at[y], 7, in_outer(i), rep))
-    loads[7].wait()
-    drain(send1, GROUP - 1, 0, 0)
-    drain(send2, outer - 1, 1, 0)
-    drain(found, ent - 1, 2, 0)
-    drain(outgoing, ent - 1, 3, 0)
-    drain(part, reps - 1, 4, 0)
-    drain(s_x, reps - 1, 5, 0)
-    drain(s_g, GROUP - 1, 6, 0)
-    drain(s_y, outer - 1, 7, 1)
-    drain(s_y, outer - 1, 7, 0)
-    total = jnp.sum(s_y[...], 0)
-    total_ref[...] = total
-    norm_total = jnp.sum(total[NORM_ROW : NORM_ROW + 1, :], 1, keepdims=True)
-    target = 0.25 * run_ref[...] + 0.75 * norm_total / (rows * ent)
-    three = upd.at[:, pl.ds(0, (reps - 1) * piece)]
-    pltpu.make_async_copy(three, three, dma.at[16]).wait()
-    pltpu.make_async_copy(three, three, dma.at[17]).wait()
+    n_a[pl.ds(rep * outer + y, 1)] = n_here[pl.ds(0, 1)]
+    loop(1, reps * outer, lambda i: remote(n_here.at[0], n_a.at[rep * outer + y], 9, in_outer(i), (rep + i // outer) % reps))
+    right, left = (rep + 1) % reps, (rep + reps - 1) % reps
+    upper, lower = pl.ds(0, half), pl.ds(half, width - half)
+
+    def pass_on(at, r, which, to):
+        remote(upd.at[at, columns(r)], upd.at[at, columns(r)], which, me, to)
+
+    def arrived(at, r, which, side):
+        ref = upd.at[at, columns(r)]
+        pltpu.make_async_copy(ref, ref, dma.at[2 * which + side]).wait()
+
+    everything = pl.ds(0, width)
+    pass_on(everything, rep, 8, right)
+    pass_on(everything, rep, 13, left)
+    drain(f_g, GROUP - 1, 6, 1)
+    f_here[2] = jnp.sum(f_g[...], 0)
+    f_y[pl.ds(y, 1)] = f_here[pl.ds(2, 1)]
+    loop(1, outer, lambda i: remote(f_here.at[2], f_y.at[y], 7, in_outer(i), rep))
+    arrived(everything, left, 8, 1)
+    pass_on(upper, left, 14, right)
+    arrived(everything, right, 13, 1)
+    pass_on(lower, right, 15, left)
+    drain(n_a, reps * outer - 1, 9, 1)
+    n_here[1] = jnp.sum(n_a[...], 0)
+    n_b[pl.ds(g, 1)] = n_here[pl.ds(1, 1)]
+    loop(1, GROUP, lambda i: remote(n_here.at[1], n_b.at[g], 10, in_group(i), rep))
+    far = (rep + 2) % reps
+    arrived(upper, far, 14, 1)
+    arrived(lower, far, 15, 1)
     updated = upd[...]
     norm = jnp.sqrt(jnp.sum(updated * updated, 0, keepdims=True) + norm_eps)
+    loads[7].wait()
+    drain(f_y, outer - 1, 7, 1)
+    total_ref[...] = jnp.sum(f_y[...], 0)
+    drain(send1, outer - 1, 0, 0)
+    drain(got2, GROUP - 1, 1, 0)
+    drain(found, ent - 1, 2, 0)
+    drain(out_a, ent - 1, 3, 0)
+    drain(out_b, ent - 1, 11, 0)
+    drain(part_a, reps - 1, 4, 0)
+    drain(part_b, reps - 1, 12, 0)
+    drain(f_x, reps - 1, 5, 0)
+    drain(f_g, GROUP - 1, 6, 0)
+    drain(f_y, outer - 1, 7, 0)
+    arrived(everything, rep, 8, 0)
+    arrived(everything, rep, 13, 0)
+    arrived(upper, left, 14, 0)
+    arrived(lower, right, 15, 0)
+    drain(n_a, reps * outer - 1, 9, 0)
+    drain(n_b, GROUP - 1, 10, 1)
+    drain(n_b, GROUP - 1, 10, 0)
+    norm_total = jnp.sum(jnp.sum(n_b[...], 0), 1, keepdims=True)
+    target = 0.25 * run_ref[...] + 0.75 * norm_total / (rows * ent)
     out_ref[...] = updated * jnp.where(rare_v[...].reshape(1, rows) == 1, target / norm, 1.0)
 
 
@@ -291,7 +362,8 @@
     piece, outer = rows // reps, ent // GROUP
     vmem, hbm = pl.BlockSpec(memory_space=pltpu.VMEM), pl.BlockSpec(memory_space=pltpu.HBM)
     v = pltpu.VMEM
-    exchange = v((ent, CAP, width), F32)
+    wide = GROUP * outer * CAP
+    exchange, first, second = v((ent, CAP + 3, 128), F32), v((ent, CAP, 128), F32), v((ent, 3, 128), F32)
     return pl.pallas_call(
         functools.partial(step_kernel, ent, reps),
         out_shape=(jax.ShapeDtypeStruct((width, rows), F32), jax.ShapeDtypeStruct((16, 128), F32)),
@@ -299,26 +371,28 @@
         scratch_shapes=[
             v(owner.shape, I32), v(row.shape, I32), v(relid.shape, I32), v(rare.shape, I32), v((width, rows), F32),
             v(rel_t.shape, BF16), v(filt.shape, F32), v(proj_t.shape, BF16),
-            v((feats, width), BF16), v((GROUP, outer, 128), F32), v((GROUP, outer, 128), F32), v((outer, 1, 128), F32),
-            v((outer, 1, 128), F32), exchange, exchange, exchange, exchange,
+            v((feats, width), BF16), v((outer, wide // 128, 128), F32), v((outer, wide // 128, 128), F32),
+            v((wide // 128, 1, 128), F32), v((GROUP, 1, 128), F32), exchange, exchange, first, second, first, second,
             v((width, req), F32), v((width, batch), F32), v((IMG_ROWS * PITCH, batch), F32),
             v((IMG_ROWS * PITCH, batch), BF16), v((IMG_ROWS * PITCH, batch), BF16), v((BAND, 192), BF16),
             v((128, BAND), BF16), v((FILT, PER, batch), BF16), v((FILT, PER, batch), F32),
             v((HEAD_PAIRS, BAND, 2 * batch), BF16), v(((HEAD_ROWS + 2) * PITCH, batch), F32), v((BAND, 128), F32),
             v((128, 128), F32),
-            v((reps, width, piece), F32), v((reps, width, piece), F32), v((width, rows), F32), v((3, 16, 128), F32),
+            v((reps, 128, piece), F32), v((reps, width - 128, piece), F32),
+            v((reps, 128, piece), F32), v((reps, width - 128, piece), F32), v((width, rows), F32), v((3, 16, 128), F32),
             v((reps, 16, 128), F32), v((GROUP, 16, 128), F32), v((outer, 16, 128), F32),
-            pltpu.SemaphoreType.DMA((8,)), pltpu.SemaphoreType.DMA((18,))],
-        compiler_params=pltpu.CompilerParams(collective_id=0, has_side_effects=True, vmem_limit_bytes=60 << 20),
+            v((2, 1, 128), F32), v((reps * outer, 1, 128), F32), v((GROUP, 1, 128), F32),
+            pltpu.SemaphoreType.DMA((8,)), pltpu.SemaphoreType.DMA((32,))],
+        compiler_params=pltpu.CompilerParams(collective_id=0, has_side_effects=True, vmem_limit_bytes=44 << 20),
         name="step",
-    )(owner, row, relid, rare, run, table_t, rel_t, filt, proj_t)
+    )(*[pltpu.with_memory_space_constraint(a, pltpu.HBM) for a in (owner, row, relid, rare)], run, *[pltpu.with_memory_space_constraint(a, pltpu.HBM) for a in (table_t, rel_t, filt, proj_t)])
 
 
 def body(entity_table, relation_table, filters, projection, request_owner, request_row, relation_id, rare_flag, running_norm):
     ent, reps = lax.axis_size("ent"), lax.axis_size("rep")
     batch, req = relation_id.shape[0], request_row.shape[0]
     new_t, total = step(request_owner.reshape(1, req), request_row, relation_id, rare_flag, running_norm.reshape(1, 1),
-                        entity_table.T, relation_table.T, filters, projection.T, ent, reps)
+                        entity_table.T, relation_table.T, filters.T, projection.T, ent, reps)
     filter_grad = total[:9, :FILT].T / (batch * ent * reps)
     return new_t.T, filter_grad
 

time: 93.6 us -> 82.7 us (0.88)
  Pallas kernels: 87.6 us -> 80 us
  local copies, waits for them, and re-layouts: 3.16 us -> 0.75 us
    pallas_call x1, Pallas kernels: 87.6 us -> 80 us  [step(): pl.pallas_call(functools.partial(step_kernel, ent, reps), out_shape=(jax....]
    unnamed x2 -> x1, local copies, waits for them, and re-layouts: 3.16 us -> 0.75 us
where the time goes in v3:
time: 82.7 us; the launch traced here: 82.6 us
  Pallas kernels  80 us (97%)
  between operations  1.29 us (2%)
    pallas_call x1, Pallas kernels, step(): pl.pallas_call(functools.partial(step_kernel, ent, reps), out_shape=(jax....  80 us

profile of v3, /device:TPU:1, one launch (start us, length us, event | category | flops | bytes accessed | tf_op | source)
XLA Modules:
  0.0 82.6 jit_solution(13461983219247505951)
XLA Ops:
  1.3 80.0 %step.1 = (f32[200,512]{1,0:T(8,128)S(1)}, f32[16,128]{1,0:T(8,128)S(1)}) custom-call(s32[1,320]{1,0:T(1,128)} %bitcast.15, s32[320]{0:T(512)} %refs_1_.1, s32[128]{0:T(128)} %refs_2_.1, s32[512]{0:T(512)} %refs_3_.1, f32[1,1]{1,0:T(1,128)} %bitcast.9.refs_4_, f32[200,512]{1,0:T(8,128)} %bitcast.12, bf16[200,822]{1,0:T(8,128)(2,1)} %bitcast.13, ...), custom_call_target="tpu_custom_call" | custom-call | tf_op jit(solution)/shard_map/step/pallas_call | solution.py:367
  81.2 0.6 multiply_bitcast_fusion
  81.9 0.8 copy.13

commit v4 on v3

--- a/solution.py
+++ b/solution.py
@@ -136,22 +136,12 @@
     pl.semaphore_wait(barrier, GROUP + outer + reps - 3)
     loop(1, outer, lambda i: remote(send1.at[(y + i) % outer], got1.at[y], 0, in_outer(i), rep))
     loads[2].wait()
-    loads[3].wait()
     table_high, table_low = split(table_v[...])
-    band = band_matrix(filt_v[...].T)
-    band_high, band_low = split(band)
-    lhs_v[...] = jnp.concatenate([band_high, band_high, band_low], 1)
-    bandt_v[...] = jnp.concatenate([band, band - band_high.astype(F32)], 1).T.astype(BF16)
     drain(got1, outer - 1, 0, 1)
     send2[...] = jnp.sum(got1[...], 0).reshape(wide // 128, 1, 128)
     share = GROUP * 128 // wide
     got2[pl.ds(g, 1)] = send2[pl.ds(g // share, 1)]
     loop(1, GROUP, lambda i: remote(send2.at[(g + i) % GROUP // share], got2.at[g], 1, in_group(i), rep))
-    loads[4].wait()
-    loads[5].wait()
-    img[...] = jnp.zeros(img.shape, F32)
-    strip[...] = mm(rel_v[...], one(iota((rels, batch), 0) == relid_v[...].reshape(1, batch)))
-    fill_image(img, HEAD_ROWS, strip, HEAD_ROWS)
     drain(got2, GROUP - 1, 1, 1)
     src = iota((slots, GROUP), 0) % ent
     pick = one(src % GROUP == iota((slots, GROUP), 1))
@@ -172,6 +162,16 @@
     loop(1, ent, lambda i: remote(found.at[(me + i) % ent], fetched.at[me], 2, (me + i) % ent, rep))
     fetched[pl.ds(me, 1)] = found[pl.ds(me, 1)]
 
+    loads[3].wait()
+    band = band_matrix(filt_v[...].T)
+    band_high, band_low = split(band)
+    lhs_v[...] = jnp.concatenate([band_high, band_high, band_low], 1)
+    bandt_v[...] = jnp.concatenate([band, band - band_high.astype(F32)], 1).T.astype(BF16)
+    loads[4].wait()
+    loads[5].wait()
+    img[...] = jnp.zeros(img.shape, F32)
+    strip[...] = mm(rel_v[...], one(iota((rels, batch), 0) == relid_v[...].reshape(1, batch)))
+    fill_image(img, HEAD_ROWS, strip, HEAD_ROWS)
     loads[6].wait()
 
     def turn_over(i, c):
@@ -193,6 +193,21 @@
         out = pl.ds(pl.multiple_of(q * 16, 16), 16)
         feat[:, out, :] = a.astype(BF16).reshape(FILT, 16, batch)
         dact[:, out, :] = (s + a * (1.0 - s)).reshape(FILT, 16, batch)
+
+    def conv_two(q):
+        def stack(k):
+            at = pl.ds(k * 2 * PITCH, 4 * PITCH)
+            hi, lo = hi_img[at, :], lo_img[at, :]
+            return jnp.concatenate([hi, lo, hi], 0)
+
+        v = mm(lhs_v[...], jnp.concatenate([stack(q), stack(q + 1)], 1))
+        s = sigmoid(v)
+        a = v * s
+        d = s + a * (1.0 - s)
+        for k in range(2):
+            out, lanes = pl.ds((q + k) * 16, 16), slice(k * batch, (k + 1) * batch)
+            feat[:, out, :] = a[:, lanes].astype(BF16).reshape(FILT, 16, batch)
+            dact[:, out, :] = d[:, lanes].reshape(FILT, 16, batch)
 
     loop(HEAD_PAIRS, PAIRS, conv)
     drain(fetched, ent - 1, 2, 1)
@@ -208,8 +223,8 @@
     high, low = split(img[head_at, :])
     hi_img[head_at, :] = high
     lo_img[head_at, :] = low
-    for q in range(HEAD_PAIRS):
-        conv(q)
+    for q in range(0, HEAD_PAIRS, 2):
+        conv_two(q)
     projected = mm(projt_v[...], feat[...].reshape(FILT * PER, batch))
     sig = sigmoid(projected)
     hidden = projected * sig
@@ -230,23 +245,34 @@
         d = mm(turned, grad_proj) * dact[:, out, :].reshape(BAND, batch)
         return split(d)
 
-    for q in range(HEAD_PAIRS):
-        dh, dl = back(q)
-        left_v[q] = jnp.concatenate([dh, dl], 1)
-        both = mm(bandt_v[...], dh)
-        at = pl.ds(q * 2 * PITCH, 4 * PITCH)
-        dimg[at, :] += both[:64] + both[64:] + mm(bandt_v[pl.ds(0, 64), :], dl)
-    for r in range(HEAD_ROWS):
-        strip[pl.ds(IMG_COLS * r, IMG_COLS), :] = dimg[pl.ds(PITCH * r, IMG_COLS), :]
-    val[:, pl.ds(0, batch)] = strip[...]
-    high, low = split(val[...])
-    packed = mm(hot, high[:128], NT) + mm(hot, low[:128], NT)
+    def head_back(first, last):
+        for q in range(first, last):
+            left = jnp.concatenate(back(q), 1)
+            left_v[q] = left
+            both = mm(bandt_v[...], left)
+            at = pl.ds(q * 2 * PITCH, 4 * PITCH)
+            dimg[at, :] += both[:64, :batch] + both[64:, :batch] + both[:64, batch:]
+
+    def head_rows(first, last):
+        for r in range(first, last):
+            strip[pl.ds(IMG_COLS * r, IMG_COLS), :] = dimg[pl.ds(PITCH * r, IMG_COLS), :]
+
+    cut_pair = (128 // IMG_COLS + 2) // 2
+    cut_row = 128 // IMG_COLS + 1
+    head_back(0, cut_pair)
+    head_rows(0, cut_row)
+    val[pl.ds(0, 128), pl.ds(0, batch)] = strip[pl.ds(0, 128), :]
+    high, low = split(val[pl.ds(0, 128), :])
+    packed = mm(hot, high, NT) + mm(hot, low, NT)
     for j in range(CAP):
         out_a[:, j, :] = packed[j * ent : (j + 1) * ent]
     loop(1, ent, lambda i: remote(out_a.at[(me + i) % ent], land_a.at[me], 3, (me + i) % ent, rep))
+    head_back(cut_pair, HEAD_PAIRS)
+    head_rows(cut_row, HEAD_ROWS)
+    val[pl.ds(128, tail), pl.ds(0, batch)] = strip[pl.ds(128, tail), :]
+    high, low = split(val[pl.ds(128, tail), :])
     blank = jnp.zeros((128 - tail, req), BF16)
-    packed = (mm(hot, jnp.concatenate([high[128:], blank], 0), NT)
-              + mm(hot, jnp.concatenate([low[128:], blank], 0), NT))
+    packed = (mm(hot, jnp.concatenate([high, blank], 0), NT) + mm(hot, jnp.concatenate([low, blank], 0), NT))
     for j, piece_of in enumerate(pack_tail(packed, ent, tail)):
         out_b[:, j, :] = piece_of
     loop(1, ent, lambda i: remote(out_b.at[(me + i) % ent], land_b.at[me], 11, (me + i) % ent, rep))
@@ -270,7 +296,8 @@
         shift = k // OUT_COLS * PITCH + k % OUT_COLS
         taps = taps + pltpu.roll(acc_v[pl.ds(k, FILT, stride=16), :], 128 - shift, 1)
     turn[...] = jnp.concatenate([taps, jnp.zeros((128 - FILT, 128), F32)], 0).T
-    filter_part = jnp.concatenate([turn[pl.ds(PITCH * i, 3), :] for i in range(3)] + [jnp.zeros((7, 128), F32)], 0)
+    filter_part = jnp.concatenate(
+        [sum(pltpu.roll(turn[pl.ds(PITCH * i + j, 1), :], FILT * j, 1) for j in range(3)) for i in range(3)], 0)
     f_here[0] = filter_part
     f_x[pl.ds(rep, 1)] = filter_part[None]
     loop(1, reps, lambda i: remote(f_here.at[0], f_x.at[rep], 5, me, (rep + i) % reps))
@@ -366,7 +393,7 @@
     exchange, first, second = v((ent, CAP + 3, 128), F32), v((ent, CAP, 128), F32), v((ent, 3, 128), F32)
     return pl.pallas_call(
         functools.partial(step_kernel, ent, reps),
-        out_shape=(jax.ShapeDtypeStruct((width, rows), F32), jax.ShapeDtypeStruct((16, 128), F32)),
+        out_shape=(jax.ShapeDtypeStruct((width, rows), F32), jax.ShapeDtypeStruct((3, 128), F32)),
         in_specs=[hbm] * 4 + [vmem] + [hbm] * 4, out_specs=(vmem,) * 2,
         scratch_shapes=[
             v(owner.shape, I32), v(row.shape, I32), v(relid.shape, I32), v(rare.shape, I32), v((width, rows), F32),
@@ -379,8 +406,8 @@
             v((HEAD_PAIRS, BAND, 2 * batch), BF16), v(((HEAD_ROWS + 2) * PITCH, batch), F32), v((BAND, 128), F32),
             v((128, 128), F32),
             v((reps, 128, piece), F32), v((reps, width - 128, piece), F32),
-            v((reps, 128, piece), F32), v((reps, width - 128, piece), F32), v((width, rows), F32), v((3, 16, 128), F32),
-            v((reps, 16, 128), F32), v((GROUP, 16, 128), F32), v((outer, 16, 128), F32),
+            v((reps, 128, piece), F32), v((reps, width - 128, piece), F32), v((width, rows), F32), v((3, 3, 128), F32),
+            v((reps, 3, 128), F32), v((GROUP, 3, 128), F32), v((outer, 3, 128), F32),
             v((2, 1, 128), F32), v((reps * outer, 1, 128), F32), v((GROUP, 1, 128), F32),
             pltpu.SemaphoreType.DMA((8,)), pltpu.SemaphoreType.DMA((32,))],
         compiler_params=pltpu.CompilerParams(collective_id=0, has_side_effects=True, vmem_limit_bytes=44 << 20),
@@ -393,7 +420,7 @@
     batch, req = relation_id.shape[0], request_row.shape[0]
     new_t, total = step(request_owner.reshape(1, req), request_row, relation_id, rare_flag, running_norm.reshape(1, 1),
                         entity_table.T, relation_table.T, filters.T, projection.T, ent, reps)
-    filter_grad = total[:9, :FILT].T / (batch * ent * reps)
+    filter_grad = total[:, : 3 * FILT].reshape(9, FILT).T / (batch * ent * reps)
     return new_t.T, filter_grad
 
 

time: 82.7 us -> 81.6 us (0.987)
  Pallas kernels: 80 us -> 78.7 us
    pallas_call x1, Pallas kernels: 80 us -> 78.7 us  [step(): pl.pallas_call(functools.partial(step_kernel, ent, reps), out_shape=(jax....]
where the time goes in v4:
time: 81.6 us; the launch traced here: 81.4 us
  Pallas kernels  78.7 us (96%)
  local copies, waits for them, and re-layouts  1.43 us (2%)
  between operations  1.3 us (2%)
    pallas_call x1, Pallas kernels, step(): pl.pallas_call(functools.partial(step_kernel, ent, reps), out_shape=(jax....  78.7 us

profile of v4, /device:TPU:1, one launch (start us, length us, event | category | flops | bytes accessed | tf_op | source)
XLA Modules:
  0.0 81.4 jit_solution(9216123909419599109)
XLA Ops:
  1.3 78.7 %step.1 = (f32[200,512]{1,0:T(8,128)S(1)}, f32[3,128]{1,0:T(4,128)S(1)}) custom-call(s32[1,320]{1,0:T(1,128)} %bitcast.15, s32[320]{0:T(512)} %refs_1_.1, s32[128]{0:T(128)} %refs_2_.1, s32[512]{0:T(512)} %refs_3_.1, f32[1,1]{1,0:T(1,128)} %bitcast.8.refs_4_, f32[200,512]{1,0:T(8,128)} %bitcast.11, bf16[200,822]{1,0:T(8,128)(2,1)} %bitcast.12, ...), custom_call_target="tpu_custom_call" | custom-call | tf_op jit(solution)/shard_map/step/pallas_call | solution.py:394
  80.0 0.7 div.12
  80.7 0.8 copy.13
  (1 shorter events, 0.0 us)

commit v5 on v4

--- a/solution.py
+++ b/solution.py
@@ -30,7 +30,8 @@
 
 
 def mm_hi(a, b, dims=NN):
-    return lax.dot_general(a, b, dims, precision=HI, preferred_element_type=F32)
+    (ah, al), (bh, bl) = split(a), split(b)
+    return mm(ah, bh, dims) + (mm(ah, bl, dims) + mm(al, bh, dims))
 
 
 def split(v):
@@ -77,7 +78,7 @@
 def step_kernel(ent, reps, *refs):
     (owner_h, row_h, relid_h, rare_h, run_ref, table_h, rel_h, filt_h, projt_h, out_ref, total_ref,
      owner_v, row_v, relid_v, rare_v, table_v, rel_v, filt_v, projt_v,
-     proj_v, send1, got1, send2, got2, found, fetched, out_a, out_b, land_a, land_b,
+     proj_v, send1, got1, send2, got2, found, found_b, fetched, fetched_b, out_a, out_b, land_a, land_b,
      val, strip, img, hi_img, lo_img, lhs_v, bandt_v, feat, dact, left_v, dimg, acc_v, turn,
      part_a, part_b, pland_a, pland_b, upd, f_here, f_x, f_g, f_y, n_here, n_a, n_b, load, dma) = refs
     me, rep = lax.axis_index("ent"), lax.axis_index("rep")
@@ -154,13 +155,15 @@
     picked = mm(hot_rows, table_high[:128], NT) + mm(hot_rows, table_low[:128], NT)
     for j in range(CAP):
         found[:, j, :] = picked[j * ent : (j + 1) * ent]
+    loop(1, ent, lambda i: remote(found.at[(me + i) % ent], fetched.at[me], 2, (me + i) % ent, rep))
     blank = jnp.zeros((128 - tail, rows), BF16)
     picked = (mm(hot_rows, jnp.concatenate([table_high[128:], blank], 0), NT)
               + mm(hot_rows, jnp.concatenate([table_low[128:], blank], 0), NT))
     for j, piece_of in enumerate(pack_tail(picked, ent, tail)):
-        found[:, CAP + j, :] = piece_of
-    loop(1, ent, lambda i: remote(found.at[(me + i) % ent], fetched.at[me], 2, (me + i) % ent, rep))
+        found_b[:, j, :] = piece_of
+    loop(1, ent, lambda i: remote(found_b.at[(me + i) % ent], fetched_b.at[me], 16, (me + i) % ent, rep))
     fetched[pl.ds(me, 1)] = found[pl.ds(me, 1)]
+    fetched_b[pl.ds(me, 1)] = found_b[pl.ds(me, 1)]
 
     loads[3].wait()
     band = band_matrix(filt_v[...].T)
@@ -215,15 +218,27 @@
     hot = one(iota((slots, req), 0) == slot)
     high, low = split(jnp.concatenate([fetched[:, j, :] for j in range(CAP)], 0))
     val[pl.ds(0, 128), :] = mm(high, hot, TN) + mm(low, hot, TN)
-    high, low = split(unpack_tail(fetched[:, CAP, :], fetched[:, CAP + 1, :], fetched[:, CAP + 2, :], tail))
+    full = 128 // IMG_COLS
+    early = (full - 2) // 4 * 2
+    strip[pl.ds(0, 128), :] = val[pl.ds(0, 128), pl.ds(0, batch)]
+
+    def take_rows(first, last):
+        for r in range(first, last):
+            img[pl.ds(PITCH * r, IMG_COLS), :] = strip[pl.ds(IMG_COLS * r, IMG_COLS), :]
+        at = pl.ds(PITCH * first, PITCH * (last - first))
+        high, low = split(img[at, :])
+        hi_img[at, :] = high
+        lo_img[at, :] = low
+
+    take_rows(0, full)
+    for q in range(0, early, 2):
+        conv_two(q)
+    drain(fetched_b, ent - 1, 16, 1)
+    high, low = split(unpack_tail(fetched_b[:, 0, :], fetched_b[:, 1, :], fetched_b[:, 2, :], tail))
     val[pl.ds(128, tail), :] = (mm(high, hot, TN) + mm(low, hot, TN))[:tail]
-    strip[...] = val[:, pl.ds(0, batch)]
-    fill_image(img, 0, strip, HEAD_ROWS)
-    head_at = pl.ds(0, HEAD_ROWS * PITCH)
-    high, low = split(img[head_at, :])
-    hi_img[head_at, :] = high
-    lo_img[head_at, :] = low
-    for q in range(0, HEAD_PAIRS, 2):
+    strip[pl.ds(128, tail), :] = val[pl.ds(128, tail), pl.ds(0, batch)]
+    take_rows(full, HEAD_ROWS)
+    for q in range(early, HEAD_PAIRS, 2):
         conv_two(q)
     projected = mm(projt_v[...], feat[...].reshape(FILT * PER, batch))
     sig = sigmoid(projected)
@@ -345,14 +360,14 @@
     f_here[2] = jnp.sum(f_g[...], 0)
     f_y[pl.ds(y, 1)] = f_here[pl.ds(2, 1)]
     loop(1, outer, lambda i: remote(f_here.at[2], f_y.at[y], 7, in_outer(i), rep))
+    drain(n_a, reps * outer - 1, 9, 1)
+    n_here[1] = jnp.sum(n_a[...], 0)
+    n_b[pl.ds(g, 1)] = n_here[pl.ds(1, 1)]
+    loop(1, GROUP, lambda i: remote(n_here.at[1], n_b.at[g], 10, in_group(i), rep))
     arrived(everything, left, 8, 1)
     pass_on(upper, left, 14, right)
     arrived(everything, right, 13, 1)
     pass_on(lower, right, 15, left)
-    drain(n_a, reps * outer - 1, 9, 1)
-    n_here[1] = jnp.sum(n_a[...], 0)
-    n_b[pl.ds(g, 1)] = n_here[pl.ds(1, 1)]
-    loop(1, GROUP, lambda i: remote(n_here.at[1], n_b.at[g], 10, in_group(i), rep))
     far = (rep + 2) % reps
     arrived(upper, far, 14, 1)
     arrived(lower, far, 15, 1)
@@ -364,6 +379,7 @@
     drain(send1, outer - 1, 0, 0)
     drain(got2, GROUP - 1, 1, 0)
     drain(found, ent - 1, 2, 0)
+    drain(found_b, ent - 1, 16, 0)
     drain(out_a, ent - 1, 3, 0)
     drain(out_b, ent - 1, 11, 0)
     drain(part_a, reps - 1, 4, 0)
@@ -390,7 +406,7 @@
     vmem, hbm = pl.BlockSpec(memory_space=pltpu.VMEM), pl.BlockSpec(memory_space=pltpu.HBM)
     v = pltpu.VMEM
     wide = GROUP * outer * CAP
-    exchange, first, second = v((ent, CAP + 3, 128), F32), v((ent, CAP, 128), F32), v((ent, 3, 128), F32)
+    first, second = v((ent, CAP, 128), F32), v((ent, 3, 128), F32)
     return pl.pallas_call(
         functools.partial(step_kernel, ent, reps),
         out_shape=(jax.ShapeDtypeStruct((width, rows), F32), jax.ShapeDtypeStruct((3, 128), F32)),
@@ -399,7 +415,7 @@
             v(owner.shape, I32), v(row.shape, I32), v(relid.shape, I32), v(rare.shape, I32), v((width, rows), F32),
             v(rel_t.shape, BF16), v(filt.shape, F32), v(proj_t.shape, BF16),
             v((feats, width), BF16), v((outer, wide // 128, 128), F32), v((outer, wide // 128, 128), F32),
-            v((wide // 128, 1, 128), F32), v((GROUP, 1, 128), F32), exchange, exchange, first, second, first, second,
+            v((wide // 128, 1, 128), F32), v((GROUP, 1, 128), F32), first, second, first, second, first, second, first, second,
             v((width, req), F32), v((width, batch), F32), v((IMG_ROWS * PITCH, batch), F32),
             v((IMG_ROWS * PITCH, batch), BF16), v((IMG_ROWS * PITCH, batch), BF16), v((BAND, 192), BF16),
             v((128, BAND), BF16), v((FILT, PER, batch), BF16), v((FILT, PER, batch), F32),
@@ -409,7 +425,7 @@
             v((reps, 128, piece), F32), v((reps, width - 128, piece), F32), v((width, rows), F32), v((3, 3, 128), F32),
             v((reps, 3, 128), F32), v((GROUP, 3, 128), F32), v((outer, 3, 128), F32),
             v((2, 1, 128), F32), v((reps * outer, 1, 128), F32), v((GROUP, 1, 128), F32),
-            pltpu.SemaphoreType.DMA((8,)), pltpu.SemaphoreType.DMA((32,))],
+            pltpu.SemaphoreType.DMA((8,)), pltpu.SemaphoreType.DMA((34,))],
         compiler_params=pltpu.CompilerParams(collective_id=0, has_side_effects=True, vmem_limit_bytes=44 << 20),
         name="step",
     )(*[pltpu.with_memory_space_constraint(a, pltpu.HBM) for a in (owner, row, relid, rare)], run, *[pltpu.with_memory_space_constraint(a, pltpu.HBM) for a in (table_t, rel_t, filt, proj_t)])

time: 81.6 us -> 81 us (level)
  no operation moved by 1% of the time
where the time goes in v5:
time: 81 us; the launch traced here: 80.9 us
  Pallas kernels  78.2 us (97%)
  local copies, waits for them, and re-layouts  1.43 us (2%)
  between operations  1.3 us (2%)
    pallas_call x1, Pallas kernels, step(): pl.pallas_call(functools.partial(step_kernel, ent, reps), out_shape=(jax....  78.2 us

profile of v5, /device:TPU:1, one launch (start us, length us, event | category | flops | bytes accessed | tf_op | source)
XLA Modules:
  0.0 80.9 jit_solution(4910471746827119108)
XLA Ops:
  1.3 78.2 %step.1 = (f32[200,512]{1,0:T(8,128)S(1)}, f32[3,128]{1,0:T(4,128)S(1)}) custom-call(s32[1,320]{1,0:T(1,128)} %bitcast.15, s32[320]{0:T(512)} %refs_1_.1, s32[128]{0:T(128)} %refs_2_.1, s32[512]{0:T(512)} %refs_3_.1, f32[1,1]{1,0:T(1,128)} %bitcast.8.refs_4_, f32[200,512]{1,0:T(8,128)} %bitcast.11, bf16[200,822]{1,0:T(8,128)(2,1)} %bitcast.12, ...), custom_call_target="tpu_custom_call" | custom-call | tf_op jit(solution)/shard_map/step/pallas_call | solution.py:410
  79.5 0.7 div.12
  80.1 0.8 copy.13
  (1 shorter events, 0.0 us)
